TPU v7x, 32 devices: a whole 2x2x4 slice. The times are simulated.
32 devices in a mesh: pipe: 2 (over x), fsdp: 16 (over z, y, core).
Axes of the slice: x: 2, y: 2, z: 4, core: 2. Of those that a mesh axis runs over, the one named last changes fastest.
Arguments:
- x_in: bfloat16 [2, 4096, 1024], P(None, 'fsdp'), may hold values from -6 to 6
- cotangent: bfloat16 [2, 4096, 1024], P(None, 'fsdp'), may hold values from -6 to 6
- segment: int32 [2, 4096], P(None, 'fsdp'), may hold values from 0 to 3, never falling along the last dimension, each value on 1 to 2000 neighbouring positions
- w_qkv: bfloat16 [2, 1024, 3072], P('pipe', 'fsdp'), may hold values from -0.1875 to 0.1875
- w_out: bfloat16 [2, 1024, 1024], P('pipe', 'fsdp'), may hold values from -1 to 1
- w_up: bfloat16 [2, 1024, 4096], P('pipe', 'fsdp'), may hold values from -0.1875 to 0.1875
- w_down: bfloat16 [2, 4096, 1024], P('pipe', 'fsdp'), may hold values from -0.09375 to 0.09375
- vectors: bfloat16 [2, 10240], P('pipe', 'fsdp'), may hold values from -3 to 3
- gains: bfloat16 [2, 2048], P('pipe', 'fsdp'), may hold values from 0.5 to 1.5
Outputs:
- section_out: bfloat16 [2, 2, 4096, 1024], P('pipe', None, 'fsdp')
- section_in_grad: bfloat16 [2, 2, 4096, 1024], P('pipe', None, 'fsdp')
- grad_w_qkv: float32 [2, 1024, 3072], P('pipe', 'fsdp')
- grad_w_out: float32 [2, 1024, 1024], P('pipe', 'fsdp')
- grad_w_up: float32 [2, 1024, 4096], P('pipe', 'fsdp')
- grad_w_down: float32 [2, 4096, 1024], P('pipe', 'fsdp')
- grad_vectors: float32 [2, 10240], P('pipe', 'fsdp')
- grad_gains: float32 [2, 2048], P('pipe', 'fsdp')
Inputs may be any that keep to these rules, and one draw needn't show every extreme that they name: `segment`: in each micro-batch the ids never fall; every document has 1 to 2000 tokens and one has exactly 2000.
All inputs are finite; a program needn't handle non-finite values.
Results may differ from a plain program's by a relative error of at most 0.015.
Values may be sent and summed in bfloat16 or wider, within the bound.
No kernel may reach another device: no remote copies, remote signals or barrier semaphores. Data moves between devices by JAX's collectives and lax.ppermute only.
A program may use at most 256 MiB of HBM per device.

v0:
```python
import jax
import jax.numpy as jnp
from jax import lax
from jax.sharding import PartitionSpec as P

H = 16
HD = 64
DOC_MAX = 2000


EPSILON = 1e-05
MASKED_SCORE = -1e30


def carried_in(value, axis, join, neutral):
    count, mine = (lax.axis_size(axis), lax.axis_index(axis))
    pieces = jax.tree.map(lambda part: lax.all_gather(part, axis), value)
    so_far = jax.tree.map(
        lambda part, zero: jnp.full_like(part, 0) + jnp.asarray(zero, part.dtype), value, neutral
    )

    def lap(position, so_far):
        longer = join(so_far, jax.tree.map(lambda part: part[position], pieces))
        return jax.tree.map(lambda new, old: jnp.where(position < mine, new, old), longer, so_far)

    return lax.fori_loop(0, count - 1, lap, so_far)


def from_behind(block, axis, distance):
    devices = range(lax.axis_size(axis))
    route = [(i - distance, i) for i in devices if i - distance in devices]
    return lax.ppermute(block, axis, route)


def gelu_tanh(values):
    return jax.nn.gelu(values, approximate=True)


def layer_norm(features, scale_vec, shift_vec):
    row_mean = jnp.mean(features, axis=-1, keepdims=True)
    centred = features - row_mean
    scaled = lax.rsqrt(jnp.mean(centred * centred, axis=-1, keepdims=True) + EPSILON)
    normed = centred * scaled
    return (normed * scale_vec + shift_vec, normed, scaled)


def norm_back(incoming, normed, scaled, scale_vec):
    dnormed = incoming * scale_vec
    inner_term = (
        dnormed
        - jnp.mean(dnormed, axis=-1, keepdims=True)
        - normed * jnp.mean(dnormed * normed, axis=-1, keepdims=True)
    )
    return (scaled * inner_term, jnp.sum(incoming * normed, axis=0), jnp.sum(incoming, axis=0))


def doc_starts(segment, fsdp_index):
    batches, tokens = segment.shape
    positions = jnp.arange(tokens, dtype=jnp.int32)
    same_doc = segment[:, :, None] == segment[:, None, :]
    first_local = (
        jnp.min(jnp.where(same_doc, positions[None, None, :], tokens), axis=2) + fsdp_index * tokens
    )
    tail_seg = segment[:, tokens - 1]
    tail_start = first_local[:, tokens - 1]

    def combine(earlier, following):
        is_empty = following[0] < 0
        joined = is_empty | (following[0] == earlier[0])
        return (
            jnp.where(is_empty, earlier[0], following[0]),
            jnp.where(joined, earlier[1], following[1]),
        )

    identity = (jnp.full((batches,), -1, jnp.int32), jnp.zeros((batches,), jnp.int32))
    prior_seg, prior_start = carried_in((tail_seg, tail_start), "fsdp", combine, identity)
    return jnp.where(segment == prior_seg[:, None], prior_start[:, None], first_local)


def block_of(key_blocks, block_index):
    return lax.dynamic_index_in_dim(key_blocks, block_index, 0, keepdims=False)


def block_scores(query_heads, key_value, block_index, starts, fsdp_index):
    tokens = query_heads.shape[0]
    key_heads = key_value[:, : H * HD].reshape(tokens, H, HD)
    scores = jnp.einsum(
        "thd,uhd->htu", query_heads, key_heads, preferred_element_type=jnp.float32
    ) * HD ** (-0.5)
    positions = jnp.arange(tokens, dtype=jnp.int32)
    key_place = (fsdp_index - block_index) * tokens + positions
    query_place = fsdp_index * tokens + positions
    allowed = (key_place[None, :] >= starts[:, None]) & (key_place[None, :] <= query_place[:, None])
    return (scores, allowed[None])


def collect_forward(key_value, block_count):
    key_blocks = jnp.zeros((block_count,) + key_value.shape, key_value.dtype)
    key_blocks = lax.dynamic_update_index_in_dim(key_blocks, key_value, 0, 0)

    def step_along(block_index, loop_state):
        moving, blocks_now = loop_state
        moving = from_behind(moving, "fsdp", 1)
        return (moving, lax.dynamic_update_index_in_dim(blocks_now, moving, block_index, 0))

    return lax.fori_loop(1, block_count, step_along, (key_value, key_blocks))[1]


def collect_backward(key_value, block_count):
    key_blocks = jnp.zeros((block_count,) + key_value.shape, key_value.dtype)
    key_blocks = lax.dynamic_update_index_in_dim(key_blocks, key_value, 0, 0)

    def step_along(block_index, loop_state):
        moving, blocks_now = loop_state
        moving = from_behind(moving, "fsdp", 1)
        return (moving, lax.dynamic_update_index_in_dim(blocks_now, moving, block_index, 0))

    return lax.fori_loop(1, block_count, step_along, (key_value, key_blocks))[1]


def attend(query_heads, key_blocks, starts, fsdp_index):
    block_count = key_blocks.shape[0]
    tokens = query_heads.shape[0]

    def measure(block_index, loop_state):
        row_max, row_total = loop_state
        scores, allowed = block_scores(
            query_heads, block_of(key_blocks, block_index), block_index, starts, fsdp_index
        )
        masked = jnp.where(allowed, scores, MASKED_SCORE)
        raised = jnp.maximum(row_max, jnp.max(masked, axis=2))
        weights = jnp.where(allowed, jnp.exp(masked - raised[:, :, None]), 0.0)
        return (raised, row_total * jnp.exp(row_max - raised) + jnp.sum(weights, axis=2))

    initial = (
        jnp.full((H, tokens), MASKED_SCORE, jnp.float32),
        jnp.zeros((H, tokens), jnp.float32),
    )
    row_max, row_total = lax.fori_loop(0, block_count, measure, initial)
    log_total = row_max + jnp.log(row_total)

    def blend(block_index, accumulated):
        key_value = block_of(key_blocks, block_index)
        scores, allowed = block_scores(query_heads, key_value, block_index, starts, fsdp_index)
        probabilities = jnp.where(allowed, jnp.exp(scores - log_total[:, :, None]), 0.0).astype(
            jnp.bfloat16
        )
        value_heads = key_value[:, H * HD :].reshape(tokens, H, HD)
        return accumulated + jnp.einsum(
            "htu,uhd->thd", probabilities, value_heads, preferred_element_type=jnp.float32
        )

    mixed_out = lax.fori_loop(0, block_count, blend, jnp.zeros((tokens, H, HD), jnp.float32))
    return (mixed_out.reshape(tokens, H * HD).astype(jnp.bfloat16), log_total)


def attend_back(query_heads, key_blocks, mixed_grad, log_total, starts, fsdp_index):
    block_count = key_blocks.shape[0]
    tokens = query_heads.shape[0]
    grad_heads = mixed_grad.reshape(tokens, H, HD)

    def probs_at(block_index):
        key_value = block_of(key_blocks, block_index)
        scores, allowed = block_scores(query_heads, key_value, block_index, starts, fsdp_index)
        probabilities = jnp.where(allowed, jnp.exp(scores - log_total[:, :, None]), 0.0)
        value_heads = key_value[:, H * HD :].reshape(tokens, H, HD)
        dprobs = jnp.einsum(
            "thd,uhd->htu", grad_heads, value_heads, preferred_element_type=jnp.float32
        )
        return (key_value, probabilities, dprobs)

    def add_inner(block_index, inner_sum):
        unused_pair, probabilities, dprobs = probs_at(block_index)
        return inner_sum + jnp.sum(probabilities * dprobs, axis=2)

    inner_sum = lax.fori_loop(0, block_count, add_inner, jnp.zeros((H, tokens), jnp.float32))

    def contribution(block_index, query_grad):
        key_value, probabilities, dprobs = probs_at(block_index)
        score_grad = (probabilities * (dprobs - inner_sum[:, :, None])).astype(jnp.bfloat16)
        key_heads = key_value[:, : H * HD].reshape(tokens, H, HD)
        query_grad = query_grad + jnp.einsum(
            "htu,uhd->thd", score_grad, key_heads, preferred_element_type=jnp.float32
        ) * HD ** (-0.5)
        key_grad = jnp.einsum(
            "htu,thd->uhd", score_grad, query_heads, preferred_element_type=jnp.float32
        ) * HD ** (-0.5)
        value_grad = jnp.einsum(
            "htu,thd->uhd",
            probabilities.astype(jnp.bfloat16),
            grad_heads,
            preferred_element_type=jnp.float32,
        )
        return (
            query_grad,
            jnp.concatenate(
                [key_grad.reshape(tokens, H * HD), value_grad.reshape(tokens, H * HD)], axis=1
            ),
        )

    query_grad, carried = contribution(block_count - 1, jnp.zeros((tokens, H, HD), jnp.float32))

    def pass_down(step_index, loop_state):
        query_grad, carried = loop_state
        carried = from_behind(carried.astype(jnp.bfloat16), "fsdp", -1).astype(carried.dtype)
        query_grad, own_part = contribution(block_count - 1 - step_index, query_grad)
        return (query_grad, carried + own_part)

    query_grad, carried = lax.fori_loop(1, block_count, pass_down, (query_grad, carried))
    return (query_grad.reshape(tokens, H * HD), carried)


def section_forward(section_input, weights, starts, fsdp_index, block_count):
    w_qkv, w_out, w_up, w_down, vectors, gains = weights
    tokens, model_width = section_input.shape
    hidden = w_up.shape[1]
    vector_f32 = vectors.astype(jnp.float32)
    gain_f32 = gains.astype(jnp.float32)
    features_in = section_input.astype(jnp.float32)
    attn_in, normed_one, scaled_one = layer_norm(
        features_in, gain_f32[:model_width], vector_f32[:model_width]
    )
    attn_low = attn_in.astype(jnp.bfloat16)
    qkv_sum = jnp.dot(attn_low, w_qkv, preferred_element_type=jnp.float32)
    query_low = (qkv_sum[:, :model_width] + vector_f32[2 * model_width : 3 * model_width]).astype(
        jnp.bfloat16
    )
    pair_bias = jnp.concatenate(
        [jnp.zeros((model_width,), jnp.float32), vector_f32[3 * model_width : 4 * model_width]]
    )
    key_value = (qkv_sum[:, model_width:] + pair_bias).astype(jnp.bfloat16)
    key_blocks = collect_forward(key_value, block_count)
    query_heads = query_low.reshape(tokens, H, HD)
    mixed_out, log_total = attend(query_heads, key_blocks, starts, fsdp_index)
    residual = features_in + (
        jnp.dot(mixed_out, w_out, preferred_element_type=jnp.float32)
        + vector_f32[4 * model_width : 5 * model_width]
    )
    ffn_in, normed_two, scaled_two = layer_norm(
        residual, gain_f32[model_width:], vector_f32[model_width : 2 * model_width]
    )
    ffn_low = ffn_in.astype(jnp.bfloat16)
    up_proj = (
        jnp.dot(ffn_low, w_up, preferred_element_type=jnp.float32)
        + vector_f32[5 * model_width : 5 * model_width + hidden]
    )
    act_low = gelu_tanh(up_proj).astype(jnp.bfloat16)
    section_result = residual + (
        jnp.dot(act_low, w_down, preferred_element_type=jnp.float32)
        + vector_f32[5 * model_width + hidden :]
    )
    kept_state = {
        "normed_one": normed_one,
        "scaled_one": scaled_one,
        "attn_low": attn_low,
        "query_heads": query_heads,
        "key_state": key_value,
        "log_total": log_total,
        "mixed_out": mixed_out,
        "normed_two": normed_two,
        "scaled_two": scaled_two,
        "ffn_low": ffn_low,
        "up_proj": up_proj,
        "act_low": act_low,
        "starts": starts,
    }
    return (section_result, kept_state)


def section_backward(incoming, kept_state, weights, fsdp_index, block_count):
    w_qkv, w_out, w_up, w_down, vectors, gains = weights
    model_width = incoming.shape[1]
    gain_f32 = gains.astype(jnp.float32)
    grad_down = jnp.einsum(
        "tf,td->fd", kept_state["act_low"], incoming, preferred_element_type=jnp.float32
    )
    down_bias = jnp.sum(incoming, axis=0, dtype=jnp.float32)
    act_grad = jnp.einsum("td,fd->tf", incoming, w_down, preferred_element_type=jnp.float32)
    unused_value, gelu_pull = jax.vjp(gelu_tanh, kept_state["up_proj"])
    up_low = gelu_pull(act_grad)[0].astype(jnp.bfloat16)
    grad_up = jnp.einsum(
        "td,tf->df", kept_state["ffn_low"], up_low, preferred_element_type=jnp.float32
    )
    up_bias = jnp.sum(up_low, axis=0, dtype=jnp.float32)
    ffn_grad = jnp.einsum("tf,df->td", up_low, w_up, preferred_element_type=jnp.float32)
    resid_norm, gain_two, shift_two = norm_back(
        ffn_grad, kept_state["normed_two"], kept_state["scaled_two"], gain_f32[model_width:]
    )
    resid_grad = incoming.astype(jnp.float32) + resid_norm
    proj_low = resid_grad.astype(jnp.bfloat16)
    grad_out = jnp.einsum(
        "te,td->ed", kept_state["mixed_out"], proj_low, preferred_element_type=jnp.float32
    )
    out_bias = jnp.sum(proj_low, axis=0, dtype=jnp.float32)
    mixed_grad = jnp.einsum(
        "td,ed->te", proj_low, w_out, preferred_element_type=jnp.float32
    ).astype(jnp.bfloat16)
    key_blocks = collect_backward(kept_state["key_state"], block_count)
    query_grad, pair_grad = attend_back(
        kept_state["query_heads"],
        key_blocks,
        mixed_grad,
        kept_state["log_total"],
        kept_state["starts"],
        fsdp_index,
    )
    qkv_low = jnp.concatenate([query_grad, pair_grad], axis=1).astype(jnp.bfloat16)
    grad_qkv = jnp.einsum(
        "td,tc->dc", kept_state["attn_low"], qkv_low, preferred_element_type=jnp.float32
    )
    qkv_bias = jnp.sum(qkv_low, axis=0, dtype=jnp.float32)
    attn_grad = jnp.einsum("tc,dc->td", qkv_low, w_qkv, preferred_element_type=jnp.float32)
    input_norm, gain_one, shift_one = norm_back(
        attn_grad, kept_state["normed_one"], kept_state["scaled_one"], gain_f32[:model_width]
    )
    input_grad = resid_grad + input_norm
    vector_grad = jnp.concatenate(
        [
            shift_one,
            shift_two,
            qkv_bias[:model_width],
            qkv_bias[2 * model_width :],
            out_bias,
            up_bias,
            down_bias,
        ]
    )
    gain_grad = jnp.concatenate([gain_one, gain_two])
    return (input_grad, (grad_qkv, grad_out, grad_up, grad_down, vector_grad, gain_grad))


def body(x_in, cotangent, segment, w_qkv, w_out, w_up, w_down, vectors, gains):
    section_index = lax.axis_index("pipe")
    fsdp_index = lax.axis_index("fsdp")
    batches, tokens, model_width = x_in.shape
    block_count = (DOC_MAX + tokens - 2) // tokens + 1
    first_section = section_index == 0
    starts_all = doc_starts(segment, fsdp_index)
    shards = (w_qkv, w_out, w_up, w_down, vectors, gains)
    gathered = (
        lax.all_gather(shards[0], "fsdp", axis=1, tiled=True),
        lax.all_gather(shards[1], "fsdp", axis=1, tiled=True),
        lax.all_gather(shards[2], "fsdp", axis=1, tiled=True),
        lax.all_gather(shards[3], "fsdp", axis=1, tiled=True),
        lax.all_gather(shards[4], "fsdp", axis=1, tiled=True),
        lax.all_gather(shards[5], "fsdp", axis=1, tiled=True),
    )
    front_weights = tuple((gathered_piece[0] for gathered_piece in gathered))
    received = jnp.zeros((tokens, model_width), jnp.bfloat16)
    saved = []
    produced = []
    for tick_index in range(batches + 1):
        own_batch = min(tick_index, batches - 1)
        prior_batch = max(tick_index - 1, 0)
        section_input = jnp.where(first_section, x_in[own_batch], received)
        starts = jnp.where(first_section, starts_all[own_batch], starts_all[prior_batch])
        result, kept_state = section_forward(
            section_input, front_weights, starts, fsdp_index, block_count
        )
        result_low = result.astype(jnp.bfloat16)
        if tick_index < batches:
            received = from_behind(result_low, "pipe", 1)
        saved.append(kept_state)
        produced.append(result_low)
    section_out = jnp.stack(
        [jnp.where(first_section, produced[batch], produced[batch + 1]) for batch in range(batches)]
    )[None]
    back_shards = (
        lax.all_gather(shards[0], "fsdp", axis=1, tiled=True),
        lax.all_gather(shards[1], "fsdp", axis=1, tiled=True),
        lax.all_gather(shards[2], "fsdp", axis=1, tiled=True),
        lax.all_gather(shards[3], "fsdp", axis=1, tiled=True),
        lax.all_gather(shards[4], "fsdp", axis=1, tiled=True),
        lax.all_gather(shards[5], "fsdp", axis=1, tiled=True),
    )
    back_weights = tuple((gathered_piece[0] for gathered_piece in back_shards))
    totals = None
    returned = jnp.zeros((tokens, model_width), jnp.bfloat16)
    sent_grads = []
    for tick_index in range(batches + 1):
        if tick_index < batches:
            upper_grad = cotangent[tick_index]
        else:
            upper_grad = jnp.zeros((tokens, model_width), jnp.bfloat16)
        incoming = jnp.where(first_section, returned, upper_grad)
        kept_state = jax.tree.map(
            lambda first_leaf, second_leaf: jnp.where(first_section, first_leaf, second_leaf),
            saved[max(tick_index - 1, 0)],
            saved[min(tick_index + 1, batches)],
        )
        input_grad, param_grads = section_backward(
            incoming, kept_state, back_weights, fsdp_index, block_count
        )
        grad_low = input_grad.astype(jnp.bfloat16)
        if tick_index < batches:
            returned = from_behind(grad_low, "pipe", -1)
        sent_grads.append(grad_low)
        if totals is None:
            totals = param_grads
        else:
            totals = jax.tree.map(jnp.add, totals, param_grads)
    totals = (
        lax.psum_scatter(totals[0], "fsdp", scatter_dimension=0, tiled=True),
        lax.psum_scatter(totals[1], "fsdp", scatter_dimension=0, tiled=True),
        lax.psum_scatter(totals[2], "fsdp", scatter_dimension=0, tiled=True),
        lax.psum_scatter(totals[3], "fsdp", scatter_dimension=0, tiled=True),
        lax.psum_scatter(totals[4], "fsdp", scatter_dimension=0, tiled=True),
        lax.psum_scatter(totals[5], "fsdp", scatter_dimension=0, tiled=True),
    )
    section_in_grad = jnp.stack(
        [
            jnp.where(first_section, sent_grads[batch + 1], sent_grads[batch])
            for batch in range(batches)
        ]
    )[None]
    return (
        section_out,
        section_in_grad,
        totals[0][None],
        totals[1][None],
        totals[2][None],
        totals[3][None],
        totals[4][None],
        totals[5][None],
    )


def solution(mesh):
    return jax.shard_map(
        body,
        mesh=mesh,
        in_specs=(
            P(None, "fsdp", None),
            P(None, "fsdp", None),
            P(None, "fsdp"),
            P("pipe", "fsdp", None),
            P("pipe", "fsdp", None),
            P("pipe", "fsdp", None),
            P("pipe", "fsdp", None),
            P("pipe", "fsdp"),
            P("pipe", "fsdp"),
        ),
        out_specs=(
            P("pipe", None, "fsdp", None),
            P("pipe", None, "fsdp", None),
            P("pipe", "fsdp", None),
            P("pipe", "fsdp", None),
            P("pipe", "fsdp", None),
            P("pipe", "fsdp", None),
            P("pipe", "fsdp"),
            P("pipe", "fsdp"),
        ),
        check_vma=False,
    )
```

profile of v0, /device:TPU:0, one launch (start us, length us, event | category | flops | bytes accessed | tf_op | source)
XLA Modules:
  0.0 2967.3 jit_solution(5210185064136262989)
XLA Ops:
  11.9 23.9 all_gather.30
  36.1 18.0 all_gather.29
  86.1 159.1 %while.298 = (s32[]{:T(128)}, bf16[256,2048]{1,0:T(8,128)(2,1)S(1)}, bf16[9,256,2048]{2,1,0:T(8,128)(2,1)}, s32[]{:T(128)}, s32[]{:T(128)}, /*index=5*/s32[]{:T(128)}) while((s32[]{:T(128)}, bf16[256,2048]{1,0:T(8,128)(2,1)S(1)}, bf16[9,256,2048]{2,1,0:T(8,128)(2,1)}, s32[]{:T(128)}, s32[]{:T(128)}, /*index=5*/s32[]{:T(128)}) %tuple.746), condition=%wide.region_3.4_spmd, body=%wide.region_2.3_spmd.sunk | while | flops 5 | bytes 8388763 | solution.py:106
  124.2 19.5 collective-permute-start
  164.2 30.5 %collective-permute-start = (bf16[256,2048]{1,0:T(8,128)(2,1)S(1)}, bf16[256,2048]{1,0:T(8,128)(2,1)S(1)}, u32[]{:S(2)}, u32[]{:S(2)}) collective-permute-start(bf16[256,2048]{1,0:T(8,128)(2,1)S(1)} %get-tuple-element.4892), channel_id=1, source_target_pairs={{0,1},{1,2},{2,3},{3,4},{4,5},{5,6},{6,7},{7,8},{8,9},{9,10},{10,1... | collective-permute-start | bytes 3145736 | tf_op jit(solution)/shard_map/while/body/eval_jaxpr/ppermute | solution.py:32
  198.1 26.5 collective-permute-start
  258.8 68.9 %while.308 = (s32[]{:T(128)}, f32[16,256]{1,0:T(8,128)S(1)}, f32[16,256]{1,0:T(8,128)S(1)}, s32[]{:T(128)}, s32[256]{0:T(256)S(1)}, /*index=5*/s32[]{:T(128)}, b...) while((s32[]{:T(128)}, f32[16,256]{1,0:T(8,128)S(1)}, ...), condition=%wide.region_10.11_spmd.clone, body=%wide.region_7.10_spmd.clone.sunk | while | flops 142823936 | bytes 12997796 | solution.py:139
  327.8 44.6 %while.309 = (s32[]{:T(128)}, f32[256,16,64]{0,2,1:T(8,128)}, bf16[9,256,2048]{1,2,0:T(8,128)(2,1)}, s32[]{:T(128)}, s32[256]{0:T(256)S(1)}, /*index=5*/s32[]{:T...) while((s32[]{:T(128)}, f32[256,16,64]{0,2,1:T(8,128)}, ...), condition=%wide.region_12.13_spmd.clone, body=%wide.region_11.12_spmd.clone.sunk | while | flops 273351168 | bytes 8017059 | solution.py:153
  414.0 188.6 %while.301 = (s32[]{:T(128)}, bf16[256,2048]{1,0:T(8,128)(2,1)}, bf16[9,256,2048]{2,1,0:T(8,128)(2,1)}, s32[]{:T(128)}, s32[]{:T(128)}, /*index=5*/s32[]{:T(128)}) while((s32[]{:T(128)}, bf16[256,2048]{1,0:T(8,128)(2,1)}, bf16[9,256,2048]{2,1,0:T(8,128)(2,1)}, s32[]{:T(128)}, s32[]{:T(128)}, /*index=5*/s32[]{:T(128)}) %tuple.832), condition=%wide.region_42.43_spmd, body=%wide.region_41.42_spmd.sunk | while | flops 5 | bytes 8388763 | solution.py:118
  414.4 38.4 %collective-permute-start.3 = (bf16[256,2048]{1,0:T(8,128)(2,1)}, bf16[256,2048]{1,0:T(8,128)(2,1)S(1)}, u32[]{:S(2)}, u32[]{:S(2)}) collective-permute-start(bf16[256,2048]{1,0:T(8,128)(2,1)} %get-tuple-element.5084), channel_id=1, source_target_pairs={{0,1},{1,2},{2,3},{3,4},{4,5},{5,6},{6,7},{7,8},{8,9},{9,10},{10,1... | collective-permute-start | bytes 3145736 | tf_op jit(solution)/shard_map/while/body/eval_jaxpr/ppermute | solution.py:32
  457.4 25.4 collective-permute-start.3
  623.4 154.0 %while.299 = (s32[]{:T(128)}, bf16[256,2048]{1,0:T(8,128)(2,1)}, bf16[9,256,2048]{2,1,0:T(8,128)(2,1)}, s32[]{:T(128)}, s32[]{:T(128)}, /*index=5*/s32[]{:T(128)}) while((s32[]{:T(128)}, bf16[256,2048]{1,0:T(8,128)(2,1)}, bf16[9,256,2048]{2,1,0:T(8,128)(2,1)}, s32[]{:T(128)}, s32[]{:T(128)}, /*index=5*/s32[]{:T(128)}) %tuple.758), condition=%wide.region_18.19_spmd, body=%wide.region_17.18_spmd.sunk | while | flops 5 | bytes 8388763 | solution.py:106
  791.3 78.0 %while.310 = (s32[]{:T(128)}, f32[16,256]{1,0:T(8,128)S(1)}, f32[16,256]{1,0:T(8,128)S(1)}, s32[]{:T(128)}, s32[256]{0:T(256)S(1)}, /*index=5*/s32[]{:T(128)}, b...) while((s32[]{:T(128)}, f32[16,256]{1,0:T(8,128)S(1)}, ...), condition=%wide.region_22.23_spmd.clone, body=%wide.region_19.22_spmd.clone.sunk | while | flops 142823936 | bytes 12997796 | solution.py:139
  869.9 46.7 %while.311 = (s32[]{:T(128)}, f32[256,16,64]{0,2,1:T(8,128)}, bf16[9,256,2048]{1,2,0:T(8,128)(2,1)}, s32[]{:T(128)}, s32[256]{0:T(256)S(1)}, /*index=5*/s32[]{:T...) while((s32[]{:T(128)}, f32[256,16,64]{0,2,1:T(8,128)}, ...), condition=%wide.region_24.25_spmd.clone, body=%wide.region_23.24_spmd.clone.sunk | while | flops 273351168 | bytes 8017059 | solution.py:153
  957.8 70.3 %while.314 = (s32[]{:T(128)}, f32[16,256]{1,0:T(8,128)S(1)}, s32[]{:T(128)}, s32[256]{0:T(256)S(1)}, s32[]{:T(128)}, /*index=5*/bf16[9,256,2048]{1,2,0:T(8,128)(...) while((s32[]{:T(128)}, f32[16,256]{1,0:T(8,128)S(1)}, ...), condition=%wide.region_45.46_spmd.clone, body=%wide.region_43.45_spmd.clone.sunk | while | flops 273879552 | bytes 14898347 | solution.py:176
  1050.8 149.6 %while.302 = (s32[]{:T(128)}, f32[256,16,64]{0,2,1:T(8,128)S(1)}, bf16[256,2048]{0,1:T(8,128)(2,1)}, bf16[9,256,2048]{1,2,0:T(8,128)(2,1)}, s32[]{:T(128)}, /*in...) while((s32[]{:T(128)}, f32[256,16,64]{0,2,1:T(8,128)S(1)}, ...), condition=%wide.region_47.48_spmd, body=%wide.region_46.47_spmd.sunk | while | flops 684655104 | bytes 43767112 | solution.py:209
  1229.3 141.6 %while.303 = (s32[]{:T(128)}, bf16[256,2048]{1,0:T(8,128)(2,1)S(1)}, bf16[9,256,2048]{2,1,0:T(8,128)(2,1)}, s32[]{:T(128)}, s32[]{:T(128)}, /*index=5*/s32[]{:T(128)}) while((s32[]{:T(128)}, bf16[256,2048]{1,0:T(8,128)(2,1)S(1)}, bf16[9,256,2048]{2,1,0:T(8,128)(2,1)}, s32[]{:T(128)}, s32[]{:T(128)}, /*index=5*/s32[]{:T(128)}) %tuple.785), condition=%wide.region_53.54_spmd, body=%wide.region_52.53_spmd.sunk | while | flops 5 | bytes 8388763 | solution.py:118
  1390.6 145.5 %while.305 = (s32[]{:T(128)}, bf16[256,2048]{1,0:T(8,128)(2,1)S(1)}, bf16[9,256,2048]{2,1,0:T(8,128)(2,1)}, s32[]{:T(128)}, s32[]{:T(128)}, /*index=5*/s32[]{:T(128)}) while((s32[]{:T(128)}, bf16[256,2048]{1,0:T(8,128)(2,1)S(1)}, bf16[9,256,2048]{2,1,0:T(8,128)(2,1)}, s32[]{:T(128)}, s32[]{:T(128)}, /*index=5*/s32[]{:T(128)}) %tuple.833), condition=%wide.region_64.65_spmd, body=%wide.region_63.64_spmd.sunk | while | flops 5 | bytes 8388763 | solution.py:118
  1556.0 145.4 %while.300 = (s32[]{:T(128)}, bf16[256,2048]{1,0:T(8,128)(2,1)S(1)}, bf16[9,256,2048]{2,1,0:T(8,128)(2,1)}, s32[]{:T(128)}, s32[]{:T(128)}, /*index=5*/s32[]{:T(128)}) while((s32[]{:T(128)}, bf16[256,2048]{1,0:T(8,128)(2,1)S(1)}, bf16[9,256,2048]{2,1,0:T(8,128)(2,1)}, s32[]{:T(128)}, s32[]{:T(128)}, /*index=5*/s32[]{:T(128)}) %tuple.776), condition=%wide.region_30.31_spmd, body=%wide.region_29.30_spmd.sunk | while | flops 5 | bytes 8388763 | solution.py:106
  1714.3 68.5 %while.312 = (s32[]{:T(128)}, f32[16,256]{1,0:T(8,128)S(1)}, f32[16,256]{1,0:T(8,128)S(1)}, s32[]{:T(128)}, s32[256]{0:T(256)S(1)}, /*index=5*/s32[]{:T(128)}, b...) while((s32[]{:T(128)}, f32[16,256]{1,0:T(8,128)S(1)}, ...), condition=%wide.region_34.35_spmd.clone, body=%wide.region_31.34_spmd.clone.sunk | while | flops 142823936 | bytes 12997796 | solution.py:139
  1784.2 44.3 %while.313 = (s32[]{:T(128)}, f32[256,16,64]{0,2,1:T(8,128)}, bf16[9,256,2048]{1,2,0:T(8,128)(2,1)}, s32[]{:T(128)}, s32[256]{0:T(256)S(1)}, /*index=5*/s32[]{:T...) while((s32[]{:T(128)}, f32[256,16,64]{0,2,1:T(8,128)}, ...), condition=%wide.region_36.37_spmd.clone, body=%wide.region_35.36_spmd.clone.sunk | while | flops 273351168 | bytes 8017059 | solution.py:153
  1882.8 70.1 %while.315 = (s32[]{:T(128)}, f32[16,256]{1,0:T(8,128)S(1)}, s32[]{:T(128)}, s32[256]{0:T(256)S(1)}, s32[]{:T(128)}, /*index=5*/bf16[9,256,2048]{1,2,0:T(8,128)(...) while((s32[]{:T(128)}, f32[16,256]{1,0:T(8,128)S(1)}, ...), condition=%wide.region_56.57_spmd.clone, body=%wide.region_54.56_spmd.clone.sunk | while | flops 273879552 | bytes 14898347 | solution.py:176
  1961.2 160.0 %while.304 = (s32[]{:T(128)}, f32[256,16,64]{0,2,1:T(8,128)S(1)}, bf16[256,2048]{0,1:T(8,128)(2,1)}, bf16[9,256,2048]{1,2,0:T(8,128)(2,1)}, s32[]{:T(128)}, /*in...) while((s32[]{:T(128)}, f32[256,16,64]{0,2,1:T(8,128)S(1)}, ...), condition=%wide.region_58.59_spmd, body=%wide.region_57.58_spmd.sunk | while | flops 684655104 | bytes 43767112 | solution.py:209
  2156.9 70.2 %while.316 = (s32[]{:T(128)}, f32[16,256]{1,0:T(8,128)S(1)}, s32[]{:T(128)}, s32[256]{0:T(256)S(1)}, s32[]{:T(128)}, /*index=5*/bf16[9,256,2048]{1,2,0:T(8,128)(...) while((s32[]{:T(128)}, f32[16,256]{1,0:T(8,128)S(1)}, ...), condition=%wide.region_67.68_spmd.clone, body=%wide.region_65.67_spmd.clone.sunk | while | flops 273879552 | bytes 14898347 | solution.py:176
  2240.4 172.3 %while.306 = (s32[]{:T(128)}, f32[256,16,64]{0,2,1:T(8,128)S(1)}, bf16[256,2048]{0,1:T(8,128)(2,1)}, bf16[9,256,2048]{1,2,0:T(8,128)(2,1)}, s32[]{:T(128)}, /*in...) while((s32[]{:T(128)}, f32[256,16,64]{0,2,1:T(8,128)S(1)}, ...), condition=%wide.region_69.70_spmd, body=%wide.region_68.69_spmd.sunk | while | flops 684655104 | bytes 43767112 | solution.py:209
  2350.1 18.7 collective-permute-done.8
  2449.5 19.0 add_add_fusion.1
  2469.7 17.2 fusion.187
  2495.2 23.1 add_add_fusion
  2537.0 89.3 %all-reduce.12 = (f32[10240]{0:T(1024)S(1)}, f32[2048]{0:T(1024)S(1)}) all-reduce(f32[10240]{0:T(1024)S(1)} %add_add_fusion.4, f32[2048]{0:T(1024)S(1)} %fusion.325), channel_id=8, replica_groups=mesh['pipe'=2,'fsdp'=16] {'fsdp'}, use_global_device_ids=true, to_apply=%region_94.95.clone | all-reduce | flops 12288 | bytes 98304
  2630.6 148.5 %reduce-scatter.9.cloned.1.call-done = f32[64,4096]{1,0:T(8,128)} async-done(((f32[1024,4096]{1,0:T(8,128)}), f32[64,4096]{1,0:T(8,128)}) %reduce-scatter.9.cloned.1.call-update) | async-done | bytes 1048592 | tf_op jit(solution)/shard_map/reduce_scatter | solution.py:405
  2779.2 181.1 %reduce-scatter.11.cloned.1.call-done = f32[256,1024]{1,0:T(8,128)} async-done(((f32[4096,1024]{1,0:T(8,128)}), f32[256,1024]{1,0:T(8,128)}) %reduce-scatter.11.cloned.1.call-update) | async-done | bytes 1048592 | tf_op jit(solution)/shard_map/reduce_scatter | solution.py:406
  (1815 shorter events, 2261.0 us)
Async XLA Ops:
  7.2 67.5 %all-gather.7.cloned.1.call-start = ((), (), s32[]{:S(2)}) async-start(), calls=%async_computation.4 | async-start | bytes 6684672 | tf_op jit(solution)/shard_map/all_gather | solution.py:341
  7.9 366.0 %all-gather.9.cloned.1.call-start = ((), (), s32[]{:S(2)}) async-start(), calls=%async_computation.5 | async-start | bytes 2228224 | tf_op jit(solution)/shard_map/all_gather | solution.py:342
  8.6 368.0 %all-gather.11.cloned.1.call-start = ((), (), s32[]{:S(2)}) async-start(), calls=%async_computation.6 | async-start | bytes 8912896 | tf_op jit(solution)/shard_map/all_gather | solution.py:343
  9.4 375.2 %all-gather.13.cloned.1.call-start = ((), (), s32[]{:S(2)}) async-start(), calls=%async_computation.7 | async-start | bytes 8912896 | tf_op jit(solution)/shard_map/all_gather | solution.py:344
  10.0 2620.6 %reduce-scatter.7.cloned.1.call-start = ((), (), s32[]{:S(2)}) async-start(), calls=%async_computation.9 | async-start | bytes 4456448 | tf_op jit(solution)/shard_map/reduce_scatter | solution.py:404
  124.2 21.7 collective-permute-start
  164.2 32.7 %collective-permute-start = (bf16[256,2048]{1,0:T(8,128)(2,1)S(1)}, bf16[256,2048]{1,0:T(8,128)(2,1)S(1)}, u32[]{:S(2)}, u32[]{:S(2)}) collective-permute-start(bf16[256,2048]{1,0:T(8,128)(2,1)S(1)} %get-tuple-element.4892), channel_id=1, source_target_pairs={{0,1},{1,2},{2,3},{3,4},{4,5},{5,6},{6,7},{7,8},{8,9},{9,10},{10,1... | collective-permute-start | bytes 3145736 | tf_op jit(solution)/shard_map/while/body/eval_jaxpr/ppermute | solution.py:32
  198.1 28.7 collective-permute-start
  414.4 40.9 %collective-permute-start.3 = (bf16[256,2048]{1,0:T(8,128)(2,1)}, bf16[256,2048]{1,0:T(8,128)(2,1)S(1)}, u32[]{:S(2)}, u32[]{:S(2)}) collective-permute-start(bf16[256,2048]{1,0:T(8,128)(2,1)} %get-tuple-element.5084), channel_id=1, source_target_pairs={{0,1},{1,2},{2,3},{3,4},{4,5},{5,6},{6,7},{7,8},{8,9},{9,10},{10,1... | collective-permute-start | bytes 3145736 | tf_op jit(solution)/shard_map/while/body/eval_jaxpr/ppermute | solution.py:32
  457.4 27.8 collective-permute-start.3
  505.6 18.1 collective-permute-start.3
  681.2 17.2 collective-permute-start.1
  738.9 17.2 collective-permute-start.1
  1043.5 173.3 %collective-permute-start.10 = (bf16[256,1024]{1,0:T(8,128)(2,1)}, bf16[256,1024]{1,0:T(8,128)(2,1)}, u32[]{:S(2)}, u32[]{:S(2)}) collective-permute-start(bf16[256,1024]{1,0:T(8,128)(2,1)} %fusion.245), channel_id=1, source_target_pairs={{0,16},{1,17},{2,18},{3,19},{4,20},{5,21},{6,22},{7,23},{8,24},{9,... | collective-permute-start | bytes 1572872 | tf_op jit(solution)/shard_map/ppermute | solution.py:32
  1069.3 18.1 collective-permute-start.4
  1106.9 18.1 collective-permute-start.4
  1835.3 25.7 collective-permute-start.11
  1981.3 18.1 collective-permute-start.6
  2001.9 17.2 collective-permute-start.6
  2021.6 18.0 collective-permute-start.6
  2042.1 17.3 collective-permute-start.6
  2061.9 17.3 collective-permute-start.6
  2081.7 17.3 collective-permute-start.6
  2101.5 17.3 collective-permute-start.6
  2238.2 392.4 %reduce-scatter.5.cloned.1.call-start = ((), (), s32[]{:S(2)}) async-start(), calls=%async_computation.8 | async-start | bytes 13369344 | tf_op jit(solution)/shard_map/reduce_scatter | solution.py:403
  2258.5 18.1 collective-permute-start.8
  2296.0 19.7 collective-permute-start.8
  2317.1 23.4 collective-permute-start.8
  2341.9 27.0 collective-permute-start.8
  2370.2 22.6 collective-permute-start.8
  2429.2 349.9 %reduce-scatter.9.cloned.1.call-start = ((), (), s32[]{:S(2)}) async-start(), calls=%async_computation.10 | async-start | bytes 17825792 | tf_op jit(solution)/shard_map/reduce_scatter | solution.py:405
  2468.5 491.8 %reduce-scatter.11.cloned.1.call-start = ((), (), s32[]{:S(2)}) async-start(), calls=%async_computation.11 | async-start | bytes 17825792 | tf_op jit(solution)/shard_map/reduce_scatter | solution.py:406
  (298 other events, 14558.1 us)
Sparse Core Ops, SparseCore 0:
  10.3 64.4 all-gather.6
  76.9 41.0 all-gather.8
  120.2 86.3 all-gather.10
  208.6 84.9 all-gather.12
  2238.4 125.6 reduce-scatter.6
  2429.3 168.4 reduce-scatter.4
  2602.5 176.5 reduce-scatter.8
  2783.8 176.4 reduce-scatter.10
where the time goes:
time: 2990 us; the launch traced here: 2970 us
  starting transfers between devices  797 us (27%)
  matrix products  734 us (25%)
  waiting for transfers between devices  694 us (23%)
  local copies, waits for them, and re-layouts  389 us (13%)
  other arithmetic  185 us (6%)
  blocking collectives  141 us (5%)
    ppermute x76, starting transfers between devices, from_behind(): return lax.ppermute(block, axis, route)  797 us
    ppermute x76, waiting for transfers between devices, from_behind(): return lax.ppermute(block, axis, route)  357 us
    dot_general x81, matrix products, block_scores(): jnp.einsum('thd,uhd->htu', query_heads, key_heads, preferred_element_type...  189 us
    reduce_scatter x1, waiting for transfers between devices, body(): lax.psum_scatter(totals[3], 'fsdp', scatter_dimension=0, tiled=True)  181 us
    reduce_scatter x1, waiting for transfers between devices, body(): lax.psum_scatter(totals[2], 'fsdp', scatter_dimension=0, tiled=True)  149 us
    squeeze x108, local copies, waits for them, and re-layouts, block_of(): return lax.dynamic_index_in_dim(key_blocks, block_index, 0, keepdims=False)  143 us
    dot_general x54, matrix products, probs_at(): jnp.einsum('thd,uhd->htu', grad_heads, value_heads, preferred_element_typ...  136 us
    unnamed x2, blocking collectives  99.2 us
  transfers between devices with their start and end apart: 84, of which 77 were waited for; matrix products, arithmetic and copies ran while one was open for 18% of the time, Pallas kernels for 0%

commit v1 on v0

v1 whole, which is shorter than its diff:
```python
import functools

import jax
import jax.numpy as jnp
from jax import lax
from jax.experimental import pallas as pl
from jax.experimental.pallas import tpu as pltpu
from jax.sharding import PartitionSpec as P

H = 16
HD = 64
DOC_MAX = 2000

EPSILON = 1e-05
MASKED_SCORE = -1e30


def dot_f32(left, right):
    return jnp.dot(left, right, preferred_element_type=jnp.float32)

def forward_kernel(off, low_ref, qkv_ref, start_ref, o_ref, o32_ref, lse_ref, keys_ref):
    count, _, tokens = qkv_ref.shape

    def turn(j, carry):
        keys_ref[j] = qkv_ref[j, HD : 2 * HD, :].T
        return carry

    lax.fori_loop(0, count, turn, 0)
    sub = lax.broadcasted_iota(jnp.int32, (tokens, tokens), 0)
    lane = lax.broadcasted_iota(jnp.int32, (1, tokens), 1)

    def query_block(i, carry):
        own = i + off
        query = qkv_ref[own, 0:HD, :] * jnp.asarray(HD ** (-0.5), jnp.bfloat16)
        first = start_ref[i]
        place = own * tokens + lane

        def key_block(j, state):
            peak, total, mixed = state
            scores = dot_f32(keys_ref[j], query)
            key_place = sub + j * tokens
            allowed = (key_place >= first) & (key_place <= place)
            scores = jnp.where(allowed, scores, MASKED_SCORE)
            raised = jnp.maximum(peak, jnp.max(scores, axis=0, keepdims=True))
            weights = jnp.exp(scores - raised)
            fade = jnp.exp(peak - raised)
            total = total * fade + jnp.sum(weights, axis=0, keepdims=True)
            mixed = mixed * fade + dot_f32(qkv_ref[j, 2 * HD : 3 * HD, :], weights.astype(jnp.bfloat16))
            return raised, total, mixed

        peak, total, mixed = lax.fori_loop(
            low_ref[i],
            own + 1,
            key_block,
            (
                jnp.full((1, tokens), MASKED_SCORE, jnp.float32),
                jnp.zeros((1, tokens), jnp.float32),
                jnp.zeros((HD, tokens), jnp.float32),
            ),
        )
        out = mixed / total
        o32_ref[i] = out
        o_ref[i] = out.astype(jnp.bfloat16)
        lse_ref[i] = peak + jnp.log(total)
        return carry

    lax.fori_loop(0, count - off, query_block, 0)


def attend(qkv, starts, low, off):
    count, _, tokens = qkv.shape
    rows = count - off
    vmem = pl.BlockSpec(memory_space=pltpu.VMEM)
    return pl.pallas_call(
        functools.partial(forward_kernel, off),
        out_shape=(
            jax.ShapeDtypeStruct((rows, HD, tokens), jnp.bfloat16),
            jax.ShapeDtypeStruct((rows, HD, tokens), jnp.float32),
            jax.ShapeDtypeStruct((rows, 1, tokens), jnp.float32),
        ),
        in_specs=[pl.BlockSpec(memory_space=pltpu.SMEM), vmem, vmem],
        out_specs=(vmem, vmem, vmem),
        scratch_shapes=[pltpu.VMEM((count, tokens, HD), jnp.bfloat16)],
        name="attend",
    )(low, qkv, starts)


def backward_kernel(off, low_ref, high_ref, qkv_ref, start_ref, do_ref, o32_ref, lse_ref,
                    out_ref, keys_ref, values_ref, query_ref, grad_ref, delta_ref, dq_ref):
    count, _, tokens = qkv_ref.shape
    scale = jnp.asarray(HD ** (-0.5), jnp.bfloat16)

    def turn(j, carry):
        keys_ref[j] = qkv_ref[j, HD : 2 * HD, :].T
        values_ref[j] = qkv_ref[j, 2 * HD : 3 * HD, :].T
        return carry

    def turn_query(i, carry):
        query_ref[i] = (qkv_ref[i + off, 0:HD, :] * scale).T
        grad = do_ref[i]
        grad_ref[i] = grad.T
        delta_ref[i] = jnp.sum(grad.astype(jnp.float32) * o32_ref[i], axis=0, keepdims=True)
        dq_ref[i] = jnp.zeros((HD, tokens), jnp.float32)
        return carry

    lax.fori_loop(0, count, turn, 0)
    lax.fori_loop(0, count - off, turn_query, 0)
    sub = lax.broadcasted_iota(jnp.int32, (tokens, tokens), 0)
    lane = lax.broadcasted_iota(jnp.int32, (1, tokens), 1)

    def key_block(j, carry):
        key_place = sub + j * tokens

        def query_block(i, state):
            dk, dv = state
            query = qkv_ref[i + off, 0:HD, :] * scale
            scores = dot_f32(keys_ref[j], query)
            place = (i + off) * tokens + lane
            allowed = (key_place >= start_ref[i]) & (key_place <= place)
            probs = jnp.where(allowed, jnp.exp(scores - lse_ref[i]), 0.0)
            dprobs = dot_f32(values_ref[j], do_ref[i])
            dscores = (probs * (dprobs - delta_ref[i])).astype(jnp.bfloat16)
            dv = dv + dot_f32(probs.astype(jnp.bfloat16), grad_ref[i])
            dk = dk + dot_f32(dscores, query_ref[i])
            dq_ref[i] = dq_ref[i] + dot_f32(qkv_ref[j, HD : 2 * HD, :], dscores)
            return dk, dv

        zero = jnp.zeros((tokens, HD), jnp.float32)
        dk, dv = lax.fori_loop(jnp.maximum(j - off, 0), high_ref[j] + 1, query_block, (zero, zero))
        out_ref[j, HD : 2 * HD, :] = dk.T.astype(jnp.bfloat16)
        out_ref[j, 2 * HD : 3 * HD, :] = dv.T.astype(jnp.bfloat16)
        return carry

    lax.fori_loop(0, count, key_block, 0)

    def finish(i, carry):
        out_ref[i + off, 0:HD, :] = (dq_ref[i] * HD ** (-0.5)).astype(jnp.bfloat16)
        return carry

    lax.fori_loop(0, count - off, finish, 0)


def attend_back(qkv, starts, low, high, do, o32, lse, off):
    count, _, tokens = qkv.shape
    rows = count - off
    vmem = pl.BlockSpec(memory_space=pltpu.VMEM)
    smem = pl.BlockSpec(memory_space=pltpu.SMEM)
    return pl.pallas_call(
        functools.partial(backward_kernel, off),
        out_shape=jax.ShapeDtypeStruct((count, 3 * HD, tokens), jnp.bfloat16),
        in_specs=[smem, smem, vmem, vmem, vmem, vmem, vmem],
        out_specs=vmem,
        scratch_shapes=[
            pltpu.VMEM((count, tokens, HD), jnp.bfloat16),
            pltpu.VMEM((count, tokens, HD), jnp.bfloat16),
            pltpu.VMEM((rows, tokens, HD), jnp.bfloat16),
            pltpu.VMEM((rows, tokens, HD), jnp.bfloat16),
            pltpu.VMEM((rows, 1, tokens), jnp.float32),
            pltpu.VMEM((rows, HD, tokens), jnp.float32),
        ],
        name="attend_back",
    )(low, high, qkv, starts, do, o32, lse)


def gelu_tanh(values):
    return jax.nn.gelu(values, approximate=True)


def layer_norm(features, scale_vec, shift_vec):
    row_mean = jnp.mean(features, axis=-1, keepdims=True)
    centred = features - row_mean
    scaled = lax.rsqrt(jnp.mean(centred * centred, axis=-1, keepdims=True) + EPSILON)
    normed = centred * scaled
    return (normed * scale_vec + shift_vec, normed, scaled)


def norm_back(incoming, normed, scaled, scale_vec):
    dnormed = incoming * scale_vec
    inner_term = (
        dnormed
        - jnp.mean(dnormed, axis=-1, keepdims=True)
        - normed * jnp.mean(dnormed * normed, axis=-1, keepdims=True)
    )
    return (scaled * inner_term, jnp.sum(incoming * normed, axis=0), jnp.sum(incoming, axis=0))


def contract(left, right, left_dim, right_dim):
    dims = (((left_dim,), (right_dim,)), ((), ()))
    return lax.dot_general(left, right, dims, preferred_element_type=jnp.float32)


def swap(value):
    return lax.ppermute(value, "pipe", [(0, 1), (1, 0)])


def head_groups():
    count = lax.axis_size("fsdp")
    if count == H:
        return None
    return [list(range(first, first + H)) for first in range(0, count, H)]


def exchange(blocks):
    return lax.all_to_all(blocks, "fsdp", 0, 0, axis_index_groups=head_groups(), tiled=True)


def halo_count():
    return 0 if lax.axis_size("fsdp") == H else H


def from_group(value, distance):
    count = lax.axis_size("fsdp")
    route = [(i, i + distance * H) for i in range(count) if 0 <= i + distance * H < count]
    return lax.ppermute(value, "fsdp", route)


def doc_tables(segments, fsdp_index):
    count, tokens = segments.shape
    halo = halo_count()
    group = fsdp_index // H
    own = lax.dynamic_slice_in_dim(segments, group * H, H, 0)
    held = own
    if halo:
        before = lax.dynamic_slice_in_dim(segments, jnp.maximum(group - 1, 0) * H, H, 0)
        before = jnp.where(group > 0, before, -1)
        held = jnp.concatenate([before, own])
    held = held.reshape(1, -1)
    starts = jnp.sum((held < own.reshape(-1, 1)).astype(jnp.int32), axis=1).reshape(H, 1, tokens)
    low = starts[:, 0, 0] // tokens
    blocks = jnp.arange(halo + H, dtype=jnp.int32)
    high = jnp.sum((low[None, :] <= blocks[:, None]).astype(jnp.int32), axis=1) - 1
    return starts, low, high


def section_forward(features_in, weights, tables):
    w_qkv, w_out, w_up, w_down, vectors, gains = weights
    width = features_in.shape[1]
    tokens = features_in.shape[0]
    starts, low, high = tables
    halo = halo_count()
    attn_in, normed_one, scaled_one = layer_norm(features_in, gains[:width], vectors["ln1"])
    attn_low = attn_in.astype(jnp.bfloat16)
    bias = jnp.concatenate([vectors["q"], jnp.zeros_like(vectors["q"]), vectors["v"]])
    qkv = (contract(w_qkv, attn_low, 0, 1) + bias[:, None]).astype(jnp.bfloat16)
    qkv = qkv.reshape(3, H, HD, tokens).transpose(1, 0, 2, 3).reshape(H, 3 * HD, tokens)
    qkv = exchange(qkv)
    if halo:
        qkv = jnp.concatenate([from_group(qkv, 1), qkv])
    mixed, mixed_f32, lse = attend(qkv, starts, low, halo)
    mixed = exchange(mixed).reshape(H * HD, tokens)
    residual = features_in + (contract(mixed, w_out, 0, 0) + vectors["out"])
    ffn_in, normed_two, scaled_two = layer_norm(residual, gains[width:], vectors["ln2"])
    ffn_low = ffn_in.astype(jnp.bfloat16)
    ffn_other = swap(ffn_low)
    ffn_both = jnp.concatenate([ffn_low, ffn_other])
    up_proj = contract(ffn_both, w_up, 1, 0) + vectors["up"]
    act_low = gelu_tanh(up_proj).astype(jnp.bfloat16)
    down = contract(act_low, w_down, 1, 0)
    arrived = swap(down[tokens:].astype(jnp.bfloat16)).astype(jnp.float32)
    result = residual + (down[:tokens] + arrived + vectors["down"])
    kept = {
        "normed_one": normed_one,
        "scaled_one": scaled_one,
        "attn_low": attn_low,
        "qkv": qkv,
        "mixed": mixed,
        "mixed_f32": mixed_f32,
        "lse": lse,
        "normed_two": normed_two,
        "scaled_two": scaled_two,
        "ffn_both": ffn_both,
        "up_proj": up_proj,
        "act_low": act_low,
    }
    return result, kept


def scatter(grad):
    return lax.psum_scatter(grad.astype(jnp.bfloat16), "fsdp", scatter_dimension=0, tiled=True)


def section_backward(incoming, incoming_other, kept, weights, tables):
    w_qkv, w_out, w_up, w_down, vectors, gains = weights
    tokens, width = incoming.shape
    starts, low, high = tables
    halo = halo_count()
    both = jnp.concatenate([incoming, incoming_other])
    act_grad = contract(both, w_down, 1, 1)
    unused_value, gelu_pull = jax.vjp(gelu_tanh, kept["up_proj"])
    up_low = gelu_pull(act_grad)[0].astype(jnp.bfloat16)
    partial = contract(up_low, w_up, 1, 1)
    arrived = swap(partial[tokens:].astype(jnp.bfloat16)).astype(jnp.float32)
    ffn_grad = partial[:tokens] + arrived
    grad_down = scatter(contract(kept["act_low"], both, 0, 0))
    grad_up = contract(kept["ffn_both"], up_low, 0, 0).astype(jnp.bfloat16)
    resid_norm, gain_two, shift_two = norm_back(
        ffn_grad, kept["normed_two"], kept["scaled_two"], gains[width:]
    )
    resid_grad = incoming.astype(jnp.float32) + resid_norm
    proj_low = resid_grad.astype(jnp.bfloat16)
    mixed_grad = contract(w_out, proj_low, 1, 1).astype(jnp.bfloat16)
    mixed_grad = exchange(mixed_grad.reshape(H, HD, tokens))
    grad_out = contract(kept["mixed"], proj_low, 1, 0).astype(jnp.bfloat16)
    grad_mid = scatter(jnp.concatenate([grad_out, grad_up], axis=1))
    dqkv = attend_back(
        kept["qkv"], starts, low, high, mixed_grad, kept["mixed_f32"], kept["lse"], halo
    )
    if halo:
        behind = from_group(dqkv[:halo], -1).astype(jnp.float32)
        behind = behind.at[:, :HD].set(0.0)
        dqkv = (dqkv[halo:].astype(jnp.float32) + behind).astype(jnp.bfloat16)
    dqkv = exchange(dqkv)
    dqkv = dqkv.reshape(H, 3, HD, tokens).transpose(1, 0, 2, 3).reshape(3 * H * HD, tokens)
    attn_grad = contract(dqkv, w_qkv, 0, 1)
    grad_qkv = scatter(contract(kept["attn_low"], dqkv, 0, 1))
    qkv_bias = jnp.sum(dqkv, axis=1, dtype=jnp.float32)
    input_norm, gain_one, shift_one = norm_back(
        attn_grad, kept["normed_one"], kept["scaled_one"], gains[:width]
    )
    vector_grad = {
        "ln1": shift_one,
        "ln2": shift_two,
        "q": qkv_bias[:width],
        "v": qkv_bias[2 * width :],
        "out": jnp.sum(proj_low, axis=0, dtype=jnp.float32),
        "up": jnp.sum(up_low, axis=0, dtype=jnp.float32),
        "down": jnp.sum(incoming, axis=0, dtype=jnp.float32),
        "gains": jnp.concatenate([gain_one, gain_two]),
    }
    return resid_grad + input_norm, (grad_qkv, grad_mid, grad_down), vector_grad


def body(x_in, cotangent, segment, w_qkv, w_out, w_up, w_down, vectors, gains):
    pipe_index = lax.axis_index("pipe")
    fsdp_index = lax.axis_index("fsdp")
    count = lax.axis_size("fsdp")
    first = pipe_index == 0
    batches, tokens, width = x_in.shape
    hidden = w_up.shape[2]
    half = hidden // count // 2

    def mine(pair):
        return jnp.where(first, pair[0], pair[1])

    def other(pair):
        return jnp.where(first, pair[1], pair[0])

    def by_section(own, received):
        return jnp.where(first, own, received), jnp.where(first, received, own)

    up_halves = w_up[0].reshape(-1, count, 2, half)
    up_halves = [up_halves[:, :, side].reshape(-1, count * half) for side in range(2)]
    down_halves = [w_down[0, :half], w_down[0, half:]]
    small = jnp.concatenate([vectors[0], gains[0]])
    qkv_shards = by_section(w_qkv[0], swap(w_qkv[0]))
    mid_own = jnp.concatenate([w_out[0], mine(up_halves)], axis=1)
    mid_sent = jnp.concatenate([w_out[0], other(up_halves)], axis=1)
    mid_shards = by_section(mid_own, swap(mid_sent))
    down_shards = by_section(mine(down_halves), swap(other(down_halves)))
    small_shards = by_section(small, swap(small))

    seg_own = mine((segment[0], segment[1]))
    packed = jnp.concatenate([small_shards[0], small_shards[1], seg_own.astype(jnp.bfloat16)])
    packed = lax.all_gather(packed, "fsdp")
    lengths = small.shape[0]
    vec_rows = vectors.shape[1]
    segments = packed[:, 2 * lengths :].astype(jnp.int32)
    tables = doc_tables(segments, fsdp_index)

    def section_weights(section):
        piece = packed[:, section * lengths : (section + 1) * lengths].astype(jnp.float32)
        flat = piece[:, :vec_rows].reshape(-1)
        up_bias = flat[5 * width : 5 * width + hidden].reshape(count, 2, half)
        named = {
            "ln1": flat[:width],
            "ln2": flat[width : 2 * width],
            "q": flat[2 * width : 3 * width],
            "v": flat[3 * width : 4 * width],
            "out": flat[4 * width : 5 * width],
            "up": mine((up_bias[:, 0].reshape(-1), up_bias[:, 1].reshape(-1))),
            "down": flat[5 * width + hidden :],
        }
        gain_all = piece[:, vec_rows:].reshape(-1)
        full_qkv = lax.all_gather(qkv_shards[section], "fsdp", axis=0, tiled=True)
        full_mid = lax.all_gather(mid_shards[section], "fsdp", axis=0, tiled=True)
        full_down = lax.all_gather(down_shards[section], "fsdp", axis=0, tiled=True)
        return full_qkv, full_mid[:, :width], full_mid[:, width:], full_down, named, gain_all

    weights = [section_weights(0), section_weights(1)]
    start = mine((x_in[0], x_in[1])).astype(jnp.float32)
    result_zero, kept_zero = section_forward(start, weights[0], tables)
    low_zero = result_zero.astype(jnp.bfloat16)
    result_one, kept_one = section_forward(low_zero.astype(jnp.float32), weights[1], tables)
    low_one = result_one.astype(jnp.bfloat16)

    pair = (cotangent[0], cotangent[1])
    grad_one, params_one, vecs_one = section_backward(
        mine(pair), other(pair), kept_one, weights[1], tables
    )
    grad_one = grad_one.astype(jnp.bfloat16)
    grad_zero, params_zero, vecs_zero = section_backward(
        grad_one, swap(grad_one), kept_zero, weights[0], tables
    )
    grad_zero = grad_zero.astype(jnp.bfloat16)

    def both_batches(zero, one):
        kept_rows = mine((zero, one))
        came = swap(other((zero, one)))
        return jnp.stack([jnp.where(first, kept_rows, came), jnp.where(first, came, kept_rows)])[None]

    section_out = both_batches(low_zero, low_one)
    section_in_grad = both_batches(grad_zero, grad_one)

    def owned(zero, one):
        return mine((zero, one)), swap(other((zero, one)))

    qkv_mine, qkv_came = owned(params_zero[0], params_one[0])
    mid_mine, mid_came = owned(params_zero[1], params_one[1])
    down_mine, down_came = owned(params_zero[2], params_one[2])
    grad_qkv = qkv_mine.astype(jnp.float32) + qkv_came.astype(jnp.float32)
    grad_out = mid_mine[:, :width].astype(jnp.float32) + mid_came[:, :width].astype(jnp.float32)

    def woven(kept_half, came_half):
        return jnp.where(first, kept_half, came_half), jnp.where(first, came_half, kept_half)

    rows = w_up.shape[1]
    up_pair = woven(mid_mine[:, width:], mid_came[:, width:])
    grad_up = jnp.stack([part.reshape(rows, count, half) for part in up_pair], axis=2)
    grad_up = grad_up.reshape(rows, hidden).astype(jnp.float32)
    grad_down = jnp.concatenate(woven(down_mine, down_came)).astype(jnp.float32)

    def flat_vectors(named):
        up_half = named["up"].reshape(count, half)
        blank = jnp.zeros_like(up_half)
        up_all = jnp.stack([jnp.where(first, up_half, blank), jnp.where(first, blank, up_half)], axis=1)
        flat = jnp.concatenate(
            [named[key] for key in ("ln1", "ln2", "q", "v", "out")] + [up_all.reshape(-1), named["down"]]
        )
        return jnp.concatenate([flat.reshape(count, -1), named["gains"].reshape(count, -1)], axis=1)

    small_grads = jnp.concatenate([flat_vectors(vecs_zero), flat_vectors(vecs_one)], axis=1)
    small_grads = jnp.sum(lax.all_to_all(small_grads, "fsdp", 0, 0, tiled=True), axis=0)
    small_mine, small_came = owned(small_grads[:lengths], small_grads[lengths:])
    small_total = small_mine + small_came
    return (
        section_out,
        section_in_grad,
        grad_qkv[None],
        grad_out[None],
        grad_up[None],
        grad_down[None],
        small_total[None, :vec_rows],
        small_total[None, vec_rows:],
    )


def solution(mesh):
    return jax.shard_map(
        body,
        mesh=mesh,
        in_specs=(
            P(None, "fsdp", None),
            P(None, "fsdp", None),
            P(None, "fsdp"),
            P("pipe", "fsdp", None),
            P("pipe", "fsdp", None),
            P("pipe", "fsdp", None),
            P("pipe", "fsdp", None),
            P("pipe", "fsdp"),
            P("pipe", "fsdp"),
        ),
        out_specs=(
            P("pipe", None, "fsdp", None),
            P("pipe", None, "fsdp", None),
            P("pipe", "fsdp", None),
            P("pipe", "fsdp", None),
            P("pipe", "fsdp", None),
            P("pipe", "fsdp", None),
            P("pipe", "fsdp"),
            P("pipe", "fsdp"),
        ),
        check_vma=False,
    )
```

time: 2990 us -> 1090 us (0.36)
  starting transfers between devices: 797 us -> 85.2 us
  matrix products: 734 us -> 120 us
  local copies, waits for them, and re-layouts: 389 us -> 21.8 us
  waiting for transfers between devices: 694 us -> 457 us
  other arithmetic: 185 us -> 42.1 us
  Pallas kernels: 0 us -> 116 us
  blocking collectives: 141 us -> 229 us
    ppermute x76 -> x17, starting transfers between devices: 797 us -> 28.2 us  [swap(): return lax.ppermute(value, 'pipe', [(0, 1), (1, 0)])]
    dot_general x279 -> x24, matrix products: 734 us -> 120 us  [contract(): lax.dot_general(left, right, dims, preferred_element_type=jnp.float32)]
    ppermute x76 -> x17, waiting for transfers between devices: 357 us -> 132 us  [swap(): return lax.ppermute(value, 'pipe', [(0, 1), (1, 0)])]
    all_to_all x0 -> x4, blocking collectives: none -> 206 us  [exchange(): lax.all_to_all(blocks, 'fsdp', 0, 0, axis_index_groups=head_groups(), til...]
    squeeze x108 -> x0, local copies, waits for them, and re-layouts: 143 us -> none  [block_of(): return lax.dynamic_index_in_dim(key_blocks, block_index, 0, keepdims=False)]
    reduce_scatter x4 -> x6, waiting for transfers between devices: 330 us -> 192 us  [scatter(): lax.psum_scatter(grad.astype(jnp.bfloat16), 'fsdp', scatter_dimension=0,...]
    pallas_call x0 -> x4, Pallas kernels: none -> 116 us  [the longest x2 61.6 us: attend_back(): pl.pallas_call(functools.partial(backward_kernel, off), out_shape=jax.Sha...]
    unnamed x2 -> x0, blocking collectives: 99.2 us -> none
  transfers between devices with their start and end apart: 84 -> 34, of which waited for: 77 -> 25; matrix products, arithmetic and copies ran while one was open for 18% -> 14% of each run, Pallas kernels for 0% -> 11%
where the time goes in v1:
time: 1090 us
  waiting for transfers between devices  457 us (42%)
  blocking collectives  229 us (21%)
  matrix products  120 us (11%)
  Pallas kernels  116 us (11%)
  starting transfers between devices  85.2 us (8%)
  other arithmetic  42.1 us (4%)
  local copies, waits for them, and re-layouts  21.8 us (2%)
  between operations  15.5 us (1%)
    all_to_all x4, blocking collectives, exchange(): lax.all_to_all(blocks, 'fsdp', 0, 0, axis_index_groups=head_groups(), til...  206 us
    reduce_scatter x6, waiting for transfers between devices, scatter(): lax.psum_scatter(grad.astype(jnp.bfloat16), 'fsdp', scatter_dimension=0,...  192 us
    ppermute x17, waiting for transfers between devices, swap(): return lax.ppermute(value, 'pipe', [(0, 1), (1, 0)])  132 us
    dot_general x24, matrix products, contract(): lax.dot_general(left, right, dims, preferred_element_type=jnp.float32)  120 us
    all_to_all x4, waiting for transfers between devices, exchange(): lax.all_to_all(blocks, 'fsdp', 0, 0, axis_index_groups=head_groups(), til...  68.8 us
    pallas_call x2, Pallas kernels, attend_back(): pl.pallas_call(functools.partial(backward_kernel, off), out_shape=jax.Sha...  61.6 us
    pallas_call x2, Pallas kernels, attend(): pl.pallas_call(functools.partial(forward_kernel, off), out_shape=(jax.Sha...  54.8 us
    all_gather x2, waiting for transfers between devices, section_weights(): full_qkv = lax.all_gather(qkv_shards[section], 'fsdp', axis=0, tiled=True)  52.7 us
  transfers between devices with their start and end apart: 34, of which 25 were waited for; matrix products, arithmetic and copies ran while one was open for 14% of the time, Pallas kernels for 11%

profile of v1, /device:TPU:0, one launch (start us, length us, event | category | flops | bytes accessed | tf_op | source)
XLA Modules:
  0.0 1086.3 jit_solution(7347373140521300792)
XLA Ops:
  10.3 9.3 collective-permute-done.1
  48.0 22.9 %all-gather.1 = bf16[16,1,1792]{2,1,0:T(2,128)(2,1)S(1)} all-gather(bf16[1,1,1792]{2,1,0:T(2,128)(2,1)S(1)} %reshape.413), channel_id=2, replica_groups=mesh['pipe'=2,'fsdp'=16] {'fsdp'}, dimensions={0}, use_global_device_ids=true | all-gather | bytes 60928 | tf_op jit(solution)/shard_map/all_gather | solution.py:364
  71.1 14.1 %all-gather.9.cloned.1.call-done = bf16[1024,3072]{1,0:T(8,128)(2,1)} async-done(((bf16[64,3072]{1,0:T(8,128)(2,1)}), bf16[1024,3072]{1,0:T(8,128)(2,1)}) %all-gather.9.cloned.1.call-update) | async-done | bytes 6291472 | tf_op jit(solution)/shard_map/all_gather | solution.py:384
  95.3 9.1 convert_reduce_fusion
  105.3 34.4 %all-to-all-done.qkv_ref = bf16[16,192,256]{2,1,0:T(8,128)(2,1)S(1)} async-done(((bf16[16,192,256]{2,1,0:T(8,128)(2,1)}), bf16[16,192,256]{2,1,0:T(8,128)(2,1)S(1)}, u32[]{:S(2)}, u32[]{:S(2)}) %all-to-all-start) | async-done | bytes 1572896 | tf_op jit(solution)/shard_map/all_to_all | solution.py:204
  140.8 27.4 %attend.2 = (bf16[16,64,256]{2,1,0:T(8,128)(2,1)}, f32[16,64,256]{2,1,0:T(8,128)}, f32[16,1,256]{2,1,0:T(1,128)}) custom-call(s32[16]{0:T(128)} %and_select_fusion.low_ref, bf16[16,192,256]{2,1,0:T(8,128)(2,1)} %copy-done, s32[16,1,256]{2,1,0:T(1,128)} %bitcast.198), custom_call_target="tpu_custom_call" | custom-call | tf_op jit(solution)/shard_map/attend/pallas_call | solution.py:74
  168.2 21.5 %all-to-all-start.1 = ((bf16[16,64,256]{2,1,0:T(8,128)(2,1)}), bf16[16,64,256]{2,1,0:T(8,128)(2,1)S(1)}, u32[]{:S(2)}, u32[]{:S(2)}) async-start(bf16[16,64,256]{2,1,0:T(8,128)(2,1)} %get-tuple-element.14), calls=%async_computation.1 | async-start | bytes 1048576 | tf_op jit(solution)/shard_map/all_to_all | solution.py:204
  190.3 14.6 %all-to-all-done.1 = bf16[16,64,256]{2,1,0:T(8,128)(2,1)S(1)} async-done(((bf16[16,64,256]{2,1,0:T(8,128)(2,1)}), bf16[16,64,256]{2,1,0:T(8,128)(2,1)S(1)}, u32[]{:S(2)}, u32[]{:S(2)}) %all-to-all-start.1) | async-done | bytes 524320 | tf_op jit(solution)/shard_map/all_to_all | solution.py:204
  209.8 12.2 %collective-permute-done.3 = bf16[256,1024]{1,0:T(8,128)(2,1)} collective-permute-done((bf16[256,1024]{1,0:T(8,128)(2,1)S(1)}, bf16[256,1024]{1,0:T(8,128)(2,1)}, u32[]{:S(2)}, u32[]{:S(2)}) %collective-permute-start.3) | collective-permute-done | bytes 524320 | tf_op jit(solution)/shard_map/ppermute | solution.py:193
  238.3 11.2 %collective-permute-done.5 = bf16[256,1024]{1,0:T(8,128)(2,1)S(1)} collective-permute-done((bf16[256,1024]{1,0:T(8,128)(2,1)S(1)}, bf16[256,1024]{1,0:T(8,128)(2,1)S(1)}, u32[]{:S(2)}, u32[]{:S(2)}) %collective-permute-start.5) | collective-permute-done | bytes 524320 | tf_op jit(solution)/shard_map/ppermute | solution.py:193
  251.4 38.6 %all-gather.15.cloned.1.call-done = bf16[1024,3072]{1,0:T(8,128)(2,1)} async-done(((bf16[64,3072]{1,0:T(8,128)(2,1)}), bf16[1024,3072]{1,0:T(8,128)(2,1)}) %all-gather.15.cloned.1.call-update) | async-done | bytes 6291472 | tf_op jit(solution)/shard_map/all_gather | solution.py:384
  295.2 58.6 %all_to_all.49.qkv_ref = bf16[16,192,256]{2,1,0:T(8,128)(2,1)} all-to-all(bf16[16,192,256]{2,1,0:T(8,128)(2,1)S(1)} %bitcast.175), channel_id=1, replica_groups=mesh['pipe'=2,'fsdp'=16] {'fsdp'}, dimensions={0} | all-to-all | bytes 3145728 | tf_op jit(solution)/shard_map/all_to_all | solution.py:204
  353.8 27.4 %attend.3 = (bf16[16,64,256]{2,1,0:T(8,128)(2,1)}, f32[16,64,256]{2,1,0:T(8,128)}, f32[16,1,256]{2,1,0:T(1,128)}) custom-call(s32[16]{0:T(128)} %and_select_fusion.low_ref, bf16[16,192,256]{2,1,0:T(8,128)(2,1)} %all_to_all.49.qkv_ref, s32[16,1,256]{2,1,0:T(1,128)} %bitcast.199), custom_call_target="tpu_custom_call" | custom-call | tf_op jit(solution)/shard_map/attend/pallas_call | solution.py:74
  381.2 12.7 %all-to-all-start.3 = ((bf16[16,64,256]{2,1,0:T(8,128)(2,1)}), bf16[16,64,256]{2,1,0:T(8,128)(2,1)S(1)}, u32[]{:S(2)}, u32[]{:S(2)}) async-start(bf16[16,64,256]{2,1,0:T(8,128)(2,1)} %get-tuple-element.15), calls=%async_computation.3 | async-start | bytes 1048576 | tf_op jit(solution)/shard_map/all_to_all | solution.py:204
  393.9 14.8 %all-to-all-done.3 = bf16[16,64,256]{2,1,0:T(8,128)(2,1)S(1)} async-done(((bf16[16,64,256]{2,1,0:T(8,128)(2,1)}), bf16[16,64,256]{2,1,0:T(8,128)(2,1)S(1)}, u32[]{:S(2)}, u32[]{:S(2)}) %all-to-all-start.3) | async-done | bytes 524320 | tf_op jit(solution)/shard_map/all_to_all | solution.py:204
  417.2 10.5 collective-permute-done.6
  450.6 11.3 %collective-permute-done.9 = bf16[256,1024]{1,0:T(8,128)(2,1)S(1)} collective-permute-done((bf16[256,1024]{1,0:T(8,128)(2,1)S(1)}, bf16[256,1024]{1,0:T(8,128)(2,1)S(1)}, u32[]{:S(2)}, u32[]{:S(2)}) %collective-permute-start.9) | collective-permute-done | bytes 524320 | tf_op jit(solution)/shard_map/ppermute | solution.py:193
  467.1 12.2 %all-to-all-start.4 = ((bf16[16,64,256]{2,1,0:T(8,128)(2,1)}), bf16[16,64,256]{2,1,0:T(8,128)(2,1)}, u32[]{:S(2)}, u32[]{:S(2)}) async-start(bf16[16,64,256]{2,1,0:T(8,128)(2,1)} %bitcast.192), calls=%async_computation.4 | async-start | bytes 1048576 | tf_op jit(solution)/shard_map/all_to_all | solution.py:204
  493.6 30.8 %attend_back.2 = bf16[16,192,256]{2,1,0:T(8,128)(2,1)} custom-call(s32[16]{0:T(128)} %and_select_fusion.low_ref, s32[16]{0:T(128)} %broadcast_add_fusion.high_ref, bf16[16,192,256]{2,1,0:T(8,128)(2,1)} %all_to_all.49.qkv_ref, s32[16,1,256]{2,1,0:T(1,128)} %bitcast.200, bf16[16,64,256]{2,1,0:T(8,128)(2,1)} %all-to-all-done.4.do_ref, ...), custom_call_target="tpu_custom_call" | custom-call | tf_op jit(solution)/shard_map/attend_back/pallas_call | solution.py:148
  524.4 56.0 %all_to_all.50 = bf16[16,192,256]{2,1,0:T(8,128)(2,1)S(1)} all-to-all(bf16[16,192,256]{2,1,0:T(8,128)(2,1)} %attend_back.2), channel_id=1, replica_groups=mesh['pipe'=2,'fsdp'=16] {'fsdp'}, dimensions={0} | all-to-all | bytes 3145728 | tf_op jit(solution)/shard_map/all_to_all | solution.py:204
  589.9 12.8 %collective-permute-done.10 = bf16[256,1024]{1,0:T(8,128)(2,1)S(1)} collective-permute-done((bf16[256,1024]{1,0:T(8,128)(2,1)S(1)}, bf16[256,1024]{1,0:T(8,128)(2,1)S(1)}, u32[]{:S(2)}, u32[]{:S(2)}) %collective-permute-start.10) | collective-permute-done | bytes 524320 | tf_op jit(solution)/shard_map/ppermute | solution.py:193
  617.7 9.0 convert_reduce_fusion.2
  661.5 25.7 %all_to_all.51.do_ref = bf16[16,64,256]{2,1,0:T(8,128)(2,1)} all-to-all(bf16[16,64,256]{2,1,0:T(8,128)(2,1)S(1)} %bitcast.193), channel_id=1, replica_groups=mesh['pipe'=2,'fsdp'=16] {'fsdp'}, dimensions={0} | all-to-all | bytes 1048576 | tf_op jit(solution)/shard_map/all_to_all | solution.py:204
  687.2 30.8 %attend_back.3 = bf16[16,192,256]{2,1,0:T(8,128)(2,1)} custom-call(s32[16]{0:T(128)} %and_select_fusion.low_ref, s32[16]{0:T(128)} %broadcast_add_fusion.high_ref, bf16[16,192,256]{2,1,0:T(8,128)(2,1)} %copy-done, s32[16,1,256]{2,1,0:T(1,128)} %bitcast.201, bf16[16,64,256]{2,1,0:T(8,128)(2,1)} %all_to_all.51.do_ref, ...), custom_call_target="tpu_custom_call" | custom-call | tf_op jit(solution)/shard_map/attend_back/pallas_call | solution.py:148
  717.9 65.3 %all_to_all.52 = bf16[16,192,256]{2,1,0:T(8,128)(2,1)S(1)} all-to-all(bf16[16,192,256]{2,1,0:T(8,128)(2,1)} %attend_back.3), channel_id=1, replica_groups=mesh['pipe'=2,'fsdp'=16] {'fsdp'}, dimensions={0} | all-to-all | bytes 3145728 | tf_op jit(solution)/shard_map/all_to_all | solution.py:204
  798.4 12.5 %collective-permute-done.7 = bf16[256,1024]{1,0:T(8,128)(2,1)S(1)} collective-permute-done((bf16[256,1024]{1,0:T(8,128)(2,1)S(1)}, bf16[256,1024]{1,0:T(8,128)(2,1)S(1)}, u32[]{:S(2)}, u32[]{:S(2)}) %collective-permute-start.7) | collective-permute-done | bytes 524320 | tf_op jit(solution)/shard_map/ppermute | solution.py:193
  812.8 11.6 %collective-permute-done.8 = bf16[256,1024]{1,0:T(8,128)(2,1)S(1)} collective-permute-done((bf16[256,1024]{1,0:T(8,128)(2,1)S(1)}, bf16[256,1024]{1,0:T(8,128)(2,1)S(1)}, u32[]{:S(2)}, u32[]{:S(2)}) %collective-permute-start.8) | collective-permute-done | bytes 524320 | tf_op jit(solution)/shard_map/ppermute | solution.py:193
  839.2 9.3 all-to-all-done.8
  856.4 10.5 collective-permute-done.12
  871.9 18.8 %reduce-scatter.11.cloned.1.call-done = bf16[64,3072]{1,0:T(8,128)(2,1)} async-done(((bf16[1024,3072]{1,0:T(8,128)(2,1)}), bf16[64,3072]{1,0:T(8,128)(2,1)}) %reduce-scatter.11.cloned.1.call-update) | async-done | bytes 393232 | tf_op jit(solution)/shard_map/reduce_scatter | solution.py:279
  893.4 85.5 %reduce-scatter.9.cloned.1.call-done = bf16[64,3072]{1,0:T(8,128)(2,1)} async-done(((bf16[1024,3072]{1,0:T(8,128)(2,1)}), bf16[64,3072]{1,0:T(8,128)(2,1)}) %reduce-scatter.9.cloned.1.call-update) | async-done | bytes 393232 | tf_op jit(solution)/shard_map/reduce_scatter | solution.py:279
  978.9 88.0 %reduce-scatter.7.cloned.1.call-done = bf16[64,3072]{1,0:T(8,128)(2,1)} async-done(((bf16[1024,3072]{1,0:T(8,128)(2,1)}), bf16[64,3072]{1,0:T(8,128)(2,1)}) %reduce-scatter.7.cloned.1.call-update) | async-done | bytes 393232 | tf_op jit(solution)/shard_map/reduce_scatter | solution.py:279
  (296 shorter events, 241.2 us)
Async XLA Ops:
  7.2 78.0 %all-gather.9.cloned.1.call-start = ((), (), s32[]{:S(2)}) async-start(), calls=%async_computation.15 | async-start | bytes 6684672 | tf_op jit(solution)/shard_map/all_gather | solution.py:384
  7.2 12.4 %collective-permute-start.1 = (bf16[64,3072]{1,0:T(8,128)(2,1)}, bf16[64,3072]{1,0:T(8,128)(2,1)S(1)}, u32[]{:S(2)}, u32[]{:S(2)}) collective-permute-start(bf16[64,3072]{1,0:T(8,128)(2,1)} %bitcast.196), channel_id=1, source_target_pairs={{0,16},{16,0},{1,17},{17,1},{2,18},{18,2},{3,19},{19,3},{4,20},{20... | collective-permute-start | bytes 1179656 | tf_op jit(solution)/shard_map/ppermute | solution.py:193
  21.5 168.8 %all-gather.11.cloned.1.call-start = ((), (), s32[]{:S(2)}) async-start(), calls=%async_computation.16 | async-start | bytes 6684672 | tf_op jit(solution)/shard_map/all_gather | solution.py:385
  24.0 10.3 collective-permute-start.2
  35.4 193.4 %all-gather.13.cloned.1.call-start = ((), (), s32[]{:S(2)}) async-start(), calls=%async_computation.17 | async-start | bytes 4456448 | tf_op jit(solution)/shard_map/all_gather | solution.py:386
  35.5 6.7 collective-permute-start.4
  43.1 246.9 %all-gather.15.cloned.1.call-start = ((), (), s32[]{:S(2)}) async-start(), calls=%async_computation.18 | async-start | bytes 6684672 | tf_op jit(solution)/shard_map/all_gather | solution.py:384
  43.6 350.3 %all-gather.17.cloned.1.call-start = ((), (), s32[]{:S(2)}) async-start(), calls=%async_computation.19 | async-start | bytes 6684672 | tf_op jit(solution)/shard_map/all_gather | solution.py:385
  91.5 48.1 %all-to-all-start = ((bf16[16,192,256]{2,1,0:T(8,128)(2,1)}), bf16[16,192,256]{2,1,0:T(8,128)(2,1)S(1)}, u32[]{:S(2)}, u32[]{:S(2)}) async-start(bf16[16,192,256]{2,1,0:T(8,128)(2,1)} %bitcast.174), calls=%async_computation | async-start | bytes 3145728 | tf_op jit(solution)/shard_map/all_to_all | solution.py:204
  168.2 36.7 %all-to-all-start.1 = ((bf16[16,64,256]{2,1,0:T(8,128)(2,1)}), bf16[16,64,256]{2,1,0:T(8,128)(2,1)S(1)}, u32[]{:S(2)}, u32[]{:S(2)}) async-start(bf16[16,64,256]{2,1,0:T(8,128)(2,1)} %get-tuple-element.14), calls=%async_computation.1 | async-start | bytes 1048576 | tf_op jit(solution)/shard_map/all_to_all | solution.py:204
  189.7 245.0 %all-gather.19.cloned.1.call-start = ((), (), s32[]{:S(2)}) async-start(), calls=%async_computation.20 | async-start | bytes 4456448 | tf_op jit(solution)/shard_map/all_gather | solution.py:386
  208.1 13.8 %collective-permute-start.3 = (bf16[256,1024]{1,0:T(8,128)(2,1)S(1)}, bf16[256,1024]{1,0:T(8,128)(2,1)}, u32[]{:S(2)}, u32[]{:S(2)}) collective-permute-start(bf16[256,1024]{1,0:T(8,128)(2,1)S(1)} %add_convert_fusion.1), channel_id=1, source_target_pairs={{0,16},{16,0},{1,17},{17,1},{2,18},{18,2},{3,19},{19,3},{4,20},{20... | collective-permute-start | bytes 1572872 | tf_op jit(solution)/shard_map/ppermute | solution.py:193
  236.5 13.1 %collective-permute-start.5 = (bf16[256,1024]{1,0:T(8,128)(2,1)S(1)}, bf16[256,1024]{1,0:T(8,128)(2,1)S(1)}, u32[]{:S(2)}, u32[]{:S(2)}) collective-permute-start(bf16[256,1024]{1,0:T(8,128)(2,1)S(1)} %slice.452), channel_id=1, source_target_pairs={{0,16},{16,0},{1,17},{17,1},{2,18},{18,2},{3,19},{19,3},{4,20},{20... | collective-permute-start | bytes 1572872 | tf_op jit(solution)/shard_map/ppermute | solution.py:193
  381.2 27.5 %all-to-all-start.3 = ((bf16[16,64,256]{2,1,0:T(8,128)(2,1)}), bf16[16,64,256]{2,1,0:T(8,128)(2,1)S(1)}, u32[]{:S(2)}, u32[]{:S(2)}) async-start(bf16[16,64,256]{2,1,0:T(8,128)(2,1)} %get-tuple-element.15), calls=%async_computation.3 | async-start | bytes 1048576 | tf_op jit(solution)/shard_map/all_to_all | solution.py:204
  413.4 14.3 %collective-permute-start.6 = (bf16[256,1024]{1,0:T(8,128)(2,1)}, bf16[256,1024]{1,0:T(8,128)(2,1)}, u32[]{:S(2)}, u32[]{:S(2)}) collective-permute-start(bf16[256,1024]{1,0:T(8,128)(2,1)} %add_convert_fusion), channel_id=1, source_target_pairs={{0,16},{16,0},{1,17},{17,1},{2,18},{18,2},{3,19},{19,3},{4,20},{20... | collective-permute-start | bytes 1572872 | tf_op jit(solution)/shard_map/ppermute | solution.py:193
  448.8 13.1 %collective-permute-start.9 = (bf16[256,1024]{1,0:T(8,128)(2,1)S(1)}, bf16[256,1024]{1,0:T(8,128)(2,1)S(1)}, u32[]{:S(2)}, u32[]{:S(2)}) collective-permute-start(bf16[256,1024]{1,0:T(8,128)(2,1)S(1)} %slice.450), channel_id=1, source_target_pairs={{0,16},{16,0},{1,17},{17,1},{2,18},{18,2},{3,19},{19,3},{4,20},{20... | collective-permute-start | bytes 1572872 | tf_op jit(solution)/shard_map/ppermute | solution.py:193
  467.1 26.5 %all-to-all-start.4 = ((bf16[16,64,256]{2,1,0:T(8,128)(2,1)}), bf16[16,64,256]{2,1,0:T(8,128)(2,1)}, u32[]{:S(2)}, u32[]{:S(2)}) async-start(bf16[16,64,256]{2,1,0:T(8,128)(2,1)} %bitcast.192), calls=%async_computation.4 | async-start | bytes 1048576 | tf_op jit(solution)/shard_map/all_to_all | solution.py:204
  479.3 374.4 %reduce-scatter.17.cloned.1.call-start = ((), (), s32[]{:S(2)}) async-start(), calls=%async_computation.26 | async-start | bytes 4456448 | tf_op jit(solution)/shard_map/reduce_scatter | solution.py:279
  487.3 366.4 %reduce-scatter.15.cloned.1.call-start = ((), (), s32[]{:S(2)}) async-start(), calls=%async_computation.25 | async-start | bytes 4456448 | tf_op jit(solution)/shard_map/reduce_scatter | solution.py:279
  588.0 14.7 %collective-permute-start.10 = (bf16[256,1024]{1,0:T(8,128)(2,1)S(1)}, bf16[256,1024]{1,0:T(8,128)(2,1)S(1)}, u32[]{:S(2)}, u32[]{:S(2)}) collective-permute-start(bf16[256,1024]{1,0:T(8,128)(2,1)S(1)} %get-tuple-element.37), channel_id=1, source_target_pairs={{0,16},{16,0},{1,17},{17,1},{2,18},{18,2},{3,19},{19,3},{4,20},{20... | collective-permute-start | bytes 1572872 | tf_op jit(solution)/shard_map/ppermute | solution.py:193
  608.8 263.1 %reduce-scatter.13.cloned.1.call-start = ((), (), s32[]{:S(2)}) async-start(), calls=%async_computation.24 | async-start | bytes 6684672 | tf_op jit(solution)/shard_map/reduce_scatter | solution.py:279
  617.2 273.5 %reduce-scatter.11.cloned.1.call-start = ((), (), s32[]{:S(2)}) async-start(), calls=%async_computation.23 | async-start | bytes 6684672 | tf_op jit(solution)/shard_map/reduce_scatter | solution.py:279
  631.8 13.8 %collective-permute-start.11 = (bf16[256,1024]{1,0:T(8,128)(2,1)S(1)}, bf16[256,1024]{1,0:T(8,128)(2,1)S(1)}, u32[]{:S(2)}, u32[]{:S(2)}) collective-permute-start(bf16[256,1024]{1,0:T(8,128)(2,1)S(1)} %slice.449), channel_id=1, source_target_pairs={{0,16},{16,0},{1,17},{17,1},{2,18},{18,2},{3,19},{19,3},{4,20},{20... | collective-permute-start | bytes 1572872 | tf_op jit(solution)/shard_map/ppermute | solution.py:193
  651.6 327.2 %reduce-scatter.9.cloned.1.call-start = ((), (), s32[]{:S(2)}) async-start(), calls=%async_computation.22 | async-start | bytes 6684672 | tf_op jit(solution)/shard_map/reduce_scatter | solution.py:279
  658.0 408.9 %reduce-scatter.7.cloned.1.call-start = ((), (), s32[]{:S(2)}) async-start(), calls=%async_computation.21 | async-start | bytes 6684672 | tf_op jit(solution)/shard_map/reduce_scatter | solution.py:279
  796.9 14.0 %collective-permute-start.7 = (bf16[256,1024]{1,0:T(8,128)(2,1)S(1)}, bf16[256,1024]{1,0:T(8,128)(2,1)S(1)}, u32[]{:S(2)}, u32[]{:S(2)}) collective-permute-start(bf16[256,1024]{1,0:T(8,128)(2,1)S(1)} %slice.451), channel_id=1, source_target_pairs={{0,16},{16,0},{1,17},{17,1},{2,18},{18,2},{3,19},{19,3},{4,20},{20... | collective-permute-start | bytes 1572872 | tf_op jit(solution)/shard_map/ppermute | solution.py:193
  811.3 13.2 %collective-permute-start.8 = (bf16[256,1024]{1,0:T(8,128)(2,1)S(1)}, bf16[256,1024]{1,0:T(8,128)(2,1)S(1)}, u32[]{:S(2)}, u32[]{:S(2)}) collective-permute-start(bf16[256,1024]{1,0:T(8,128)(2,1)S(1)} %get-tuple-element.46), channel_id=1, source_target_pairs={{0,16},{16,0},{1,17},{17,1},{2,18},{18,2},{3,19},{19,3},{4,20},{20... | collective-permute-start | bytes 1572872 | tf_op jit(solution)/shard_map/ppermute | solution.py:193
  834.2 14.4 %all-to-all-start.8 = ((f32[16,1,1536]{2,1,0:T(1,128)}), f32[16,1,1536]{2,1,0:T(1,128)S(1)}, u32[]{:S(2)}, u32[]{:S(2)}) async-start(f32[16,1,1536]{2,1,0:T(1,128)} %all_to_all.38), calls=%async_computation.14 | async-start | bytes 196608 | tf_op jit(solution)/shard_map/all_to_all | solution.py:442
  852.1 14.9 %collective-permute-start.12 = (bf16[256,1024]{1,0:T(8,128)(2,1)S(1)}, bf16[256,1024]{1,0:T(8,128)(2,1)S(1)}, u32[]{:S(2)}, u32[]{:S(2)}) collective-permute-start(bf16[256,1024]{1,0:T(8,128)(2,1)S(1)} %get-tuple-element.44), channel_id=1, source_target_pairs={{0,16},{16,0},{1,17},{17,1},{2,18},{18,2},{3,19},{19,3},{4,20},{20... | collective-permute-start | bytes 1572872 | tf_op jit(solution)/shard_map/ppermute | solution.py:193
  854.7 16.0 %collective-permute-start.15 = (bf16[128,1024]{1,0:T(8,128)(2,1)S(1)}, bf16[128,1024]{1,0:T(8,128)(2,1)S(1)}, u32[]{:S(2)}, u32[]{:S(2)}) collective-permute-start(bf16[128,1024]{1,0:T(8,128)(2,1)S(1)} %broadcast_select_fusion.12), channel_id=1, source_target_pairs={{0,16},{16,0},{1,17},{17,1},{2,18},{18,2},{3,19},{19,3},{4,20},{20... | collective-permute-start | bytes 786440 | tf_op jit(solution)/shard_map/ppermute | solution.py:193
  891.9 177.6 %collective-permute-start.14 = (bf16[64,3072]{1,0:T(8,128)(2,1)S(1)}, bf16[64,3072]{1,0:T(8,128)(2,1)S(1)}, u32[]{:S(2)}, u32[]{:S(2)}) collective-permute-start(bf16[64,3072]{1,0:T(8,128)(2,1)S(1)} %get-tuple-element.63), channel_id=1, source_target_pairs={{0,16},{16,0},{1,17},{17,1},{2,18},{18,2},{3,19},{19,3},{4,20},{20... | collective-permute-start | bytes 1179656 | tf_op jit(solution)/shard_map/ppermute | solution.py:193
  1067.9 10.3 collective-permute-start.13
  (43 other events, 463.1 us)
Sparse Core Ops, SparseCore 0:
  21.7 63.5 all-gather.8
  88.1 84.1 all-gather.10
  174.4 52.6 all-gather.12
  229.8 60.0 all-gather.14
  292.6 83.1 all-gather.16
  378.4 51.8 all-gather.18
  487.4 90.3 reduce-scatter.16
  608.9 80.6 reduce-scatter.14
  693.6 108.0 reduce-scatter.12
  805.5 85.1 reduce-scatter.10
  894.6 84.2 reduce-scatter.8
  982.7 84.1 reduce-scatter.6

commit v2 on v1

--- a/solution.py
+++ b/solution.py
@@ -7,9 +7,9 @@
 from jax.experimental.pallas import tpu as pltpu
 from jax.sharding import PartitionSpec as P
 
+
 H = 16
 HD = 64
-DOC_MAX = 2000
 
 EPSILON = 1e-05
 MASKED_SCORE = -1e30
@@ -18,15 +18,20 @@
 def dot_f32(left, right):
     return jnp.dot(left, right, preferred_element_type=jnp.float32)
 
+
+STRIDE = 4
+
+
 def forward_kernel(off, low_ref, qkv_ref, start_ref, o_ref, o32_ref, lse_ref, keys_ref):
     count, _, tokens = qkv_ref.shape
+    span = STRIDE * tokens
 
     def turn(j, carry):
-        keys_ref[j] = qkv_ref[j, HD : 2 * HD, :].T
+        keys_ref[pl.ds(pl.multiple_of(j * tokens, tokens), tokens), :] = qkv_ref[j, HD : 2 * HD, :].T
         return carry
 
     lax.fori_loop(0, count, turn, 0)
-    sub = lax.broadcasted_iota(jnp.int32, (tokens, tokens), 0)
+    sub = lax.broadcasted_iota(jnp.int32, (span, tokens), 0)
     lane = lax.broadcasted_iota(jnp.int32, (1, tokens), 1)
 
     def query_block(i, carry):
@@ -34,24 +39,32 @@
         query = qkv_ref[own, 0:HD, :] * jnp.asarray(HD ** (-0.5), jnp.bfloat16)
         first = start_ref[i]
         place = own * tokens + lane
-
-        def key_block(j, state):
+        trips = (own + STRIDE - low_ref[i]) // STRIDE
+
+        def key_blocks(trip, state):
             peak, total, mixed = state
-            scores = dot_f32(keys_ref[j], query)
-            key_place = sub + j * tokens
-            allowed = (key_place >= first) & (key_place <= place)
+            block = jnp.minimum(low_ref[i] + trip * STRIDE, count - STRIDE)
+            rows = pl.multiple_of(block * tokens, tokens)
+            scores = dot_f32(keys_ref[pl.ds(rows, span), :], query)
+            key_place = sub + block * tokens
+            least = jnp.maximum(first, (low_ref[i] + trip * STRIDE) * tokens)
+            allowed = (key_place >= least) & (key_place <= place)
             scores = jnp.where(allowed, scores, MASKED_SCORE)
             raised = jnp.maximum(peak, jnp.max(scores, axis=0, keepdims=True))
             weights = jnp.exp(scores - raised)
             fade = jnp.exp(peak - raised)
             total = total * fade + jnp.sum(weights, axis=0, keepdims=True)
-            mixed = mixed * fade + dot_f32(qkv_ref[j, 2 * HD : 3 * HD, :], weights.astype(jnp.bfloat16))
+            low = weights.astype(jnp.bfloat16)
+            mixed = mixed * fade
+            for part in range(STRIDE):
+                values = qkv_ref[block + part, 2 * HD : 3 * HD, :]
+                mixed = mixed + dot_f32(values, low[part * tokens : (part + 1) * tokens])
             return raised, total, mixed
 
         peak, total, mixed = lax.fori_loop(
-            low_ref[i],
-            own + 1,
-            key_block,
+            0,
+            trips,
+            key_blocks,
             (
                 jnp.full((1, tokens), MASKED_SCORE, jnp.float32),
                 jnp.zeros((1, tokens), jnp.float32),
@@ -80,7 +93,7 @@
         ),
         in_specs=[pl.BlockSpec(memory_space=pltpu.SMEM), vmem, vmem],
         out_specs=(vmem, vmem, vmem),
-        scratch_shapes=[pltpu.VMEM((count, tokens, HD), jnp.bfloat16)],
+        scratch_shapes=[pltpu.VMEM((count * tokens, HD), jnp.bfloat16)],
         name="attend",
     )(low, qkv, starts)
 
@@ -215,7 +228,7 @@
 
 
 def doc_tables(segments, fsdp_index):
-    count, tokens = segments.shape
+    _, tokens = segments.shape
     halo = halo_count()
     group = fsdp_index // H
     own = lax.dynamic_slice_in_dim(segments, group * H, H, 0)
@@ -232,32 +245,88 @@
     return starts, low, high
 
 
-def section_forward(features_in, weights, tables):
-    w_qkv, w_out, w_up, w_down, vectors, gains = weights
+def by_head(columns, tokens):
+    return columns.reshape(3, H, HD, tokens).transpose(1, 0, 2, 3).reshape(H, 3 * HD, tokens)
+
+
+def from_heads(blocks, tokens):
+    return blocks.reshape(H, 3, HD, tokens).transpose(1, 0, 2, 3).reshape(3 * H * HD, tokens)
+
+
+def heads_from_tokens(attn_low, w_qkv, vectors):
+    bias = jnp.concatenate([vectors["q"], jnp.zeros_like(vectors["q"]), vectors["v"]])
+    qkv = (contract(w_qkv, attn_low, 0, 1) + bias[:, None]).astype(jnp.bfloat16)
+    return exchange(by_head(qkv, attn_low.shape[0]))
+
+
+def spread_head_columns(shard):
+    rows = shard.shape[0]
+    blocks = by_head(shard.T, rows)
+    copies = lax.axis_size("fsdp") // H
+    blocks = jnp.concatenate([blocks] * copies)
+    blocks = lax.all_to_all(blocks, "fsdp", 0, 0, tiled=True)
+    return blocks.transpose(1, 0, 2).reshape(3 * HD, -1)
+
+
+def collect_head_columns(grad, small):
+    count = lax.axis_size("fsdp")
+    blocks = grad.reshape(3 * HD, count, -1).transpose(1, 0, 2).astype(jnp.bfloat16)
+    rows = blocks.shape[2]
+    packed = small.astype(jnp.bfloat16).reshape(count, -1, rows)
+    blocks = jnp.concatenate([blocks, packed], axis=1)
+    blocks = lax.all_to_all(blocks, "fsdp", 0, 0, tiled=True)
+    small = jnp.sum(blocks[:, 3 * HD :].astype(jnp.float32), axis=0).reshape(-1)
+    blocks = blocks[:, : 3 * HD].reshape(count // H, H, 3 * HD, rows)
+    if count > H:
+        blocks = jnp.sum(blocks.astype(jnp.float32), axis=0).astype(jnp.bfloat16)
+    return from_heads(blocks.reshape(H, 3 * HD, rows), rows).T, small
+
+
+def heads_of_group(attn_all, w_head, vectors, head):
+    bias = jnp.stack([vectors["q"], jnp.zeros_like(vectors["q"]), vectors["v"]])
+    bias = lax.dynamic_index_in_dim(bias.reshape(3, H, HD), head, 1, keepdims=False).reshape(-1)
+    blocks, tokens, width = attn_all.shape
+    qkv = contract(w_head, attn_all.reshape(blocks * tokens, width), 1, 1) + bias[:, None]
+    return qkv.astype(jnp.bfloat16).reshape(3 * HD, blocks, tokens).transpose(1, 0, 2)
+
+
+def section_forward(features_in, normed_in, qkv, down_shard, weights, tables):
+    w_out, w_up, vectors, gains = weights
+    staged = lax.axis_size("fsdp") == H
+    attn_low, normed_one, scaled_one = normed_in
     width = features_in.shape[1]
     tokens = features_in.shape[0]
-    starts, low, high = tables
+    starts, low, _ = tables
     halo = halo_count()
-    attn_in, normed_one, scaled_one = layer_norm(features_in, gains[:width], vectors["ln1"])
-    attn_low = attn_in.astype(jnp.bfloat16)
-    bias = jnp.concatenate([vectors["q"], jnp.zeros_like(vectors["q"]), vectors["v"]])
-    qkv = (contract(w_qkv, attn_low, 0, 1) + bias[:, None]).astype(jnp.bfloat16)
-    qkv = qkv.reshape(3, H, HD, tokens).transpose(1, 0, 2, 3).reshape(H, 3 * HD, tokens)
-    qkv = exchange(qkv)
     if halo:
         qkv = jnp.concatenate([from_group(qkv, 1), qkv])
+    if staged:
+        pieces = gather_along_z(after(down_shard, qkv))
     mixed, mixed_f32, lse = attend(qkv, starts, low, halo)
-    mixed = exchange(mixed).reshape(H * HD, tokens)
+    if staged:
+        column, beside = gather_along_y([after(piece, lse) for piece in pieces])
+    mixed = exchange(after(mixed, column) if staged else mixed)
+    mixed = mixed.reshape(H * HD, tokens)
+    if staged:
+        plane, across = gather_across_cores(column, after(beside, mixed))
+    else:
+        w_down = lax.all_gather(down_shard, "fsdp", axis=0, tiled=True)
     residual = features_in + (contract(mixed, w_out, 0, 0) + vectors["out"])
     ffn_in, normed_two, scaled_two = layer_norm(residual, gains[width:], vectors["ln2"])
     ffn_low = ffn_in.astype(jnp.bfloat16)
     ffn_other = swap(ffn_low)
-    ffn_both = jnp.concatenate([ffn_low, ffn_other])
-    up_proj = contract(ffn_both, w_up, 1, 0) + vectors["up"]
-    act_low = gelu_tanh(up_proj).astype(jnp.bfloat16)
-    down = contract(act_low, w_down, 1, 0)
-    arrived = swap(down[tokens:].astype(jnp.bfloat16)).astype(jnp.float32)
-    result = residual + (down[:tokens] + arrived + vectors["down"])
+    up_own = contract(ffn_low, w_up, 1, 0) + vectors["up"]
+    act_own = gelu_tanh(up_own).astype(jnp.bfloat16)
+    if staged:
+        ffn_other, act_own, across = lax.optimization_barrier((ffn_other, act_own, across))
+        w_down = gathered_rows(plane, across)
+    else:
+        ffn_other, act_own = lax.optimization_barrier((ffn_other, act_own))
+    up_other = contract(ffn_other, w_up, 1, 0) + vectors["up"]
+    act_other = gelu_tanh(up_other).astype(jnp.bfloat16)
+    arrived = swap(contract(act_other, w_down, 1, 0).astype(jnp.bfloat16))
+    down_own = contract(act_own, w_down, 1, 0)
+    unfinished = (residual + (down_own + vectors["down"]), arrived)
     kept = {
         "normed_one": normed_one,
         "scaled_one": scaled_one,
@@ -268,40 +337,154 @@
         "lse": lse,
         "normed_two": normed_two,
         "scaled_two": scaled_two,
-        "ffn_both": ffn_both,
-        "up_proj": up_proj,
-        "act_low": act_low,
+        "ffn_both": jnp.concatenate([ffn_low, ffn_other]),
+        "up_own": up_own,
+        "up_other": up_other,
+        "act_both": jnp.concatenate([act_own, act_other]),
+        "w_down": w_down,
     }
-    return result, kept
+    return unfinished, kept
+
+
+def finish(unfinished, after):
+    own, arrived = unfinished
+    arrived, own, after = lax.optimization_barrier((arrived, own, after))
+    return own + arrived.astype(jnp.float32), after
 
 
 def scatter(grad):
     return lax.psum_scatter(grad.astype(jnp.bfloat16), "fsdp", scatter_dimension=0, tiled=True)
 
 
-def section_backward(incoming, incoming_other, kept, weights, tables):
-    w_qkv, w_out, w_up, w_down, vectors, gains = weights
+def shifted(value, axis_of, distance):
+    count = lax.axis_size("fsdp")
+    size, stride = {"z": (count // 4, 4), "y": (2, 2), "core": (2, 1)}[axis_of]
+
+    def ahead(i):
+        at = i // stride % size
+        return i + ((at + distance) % size - at) * stride
+
+    return lax.ppermute(value, "fsdp", [(i, ahead(i)) for i in range(count)])
+
+
+def places():
+    index = lax.axis_index("fsdp")
+    return index // 4, index // 2 % 2, index % 2
+
+
+def gather_along_z(shard):
+    depth = lax.axis_size("fsdp") // 4
+    return [shard] + [shifted(shard, "z", step) for step in range(1, depth)]
+
+
+def gather_along_y(pieces):
+    z, _, _ = places()
+    depth = len(pieces)
+    column = jnp.zeros((depth,) + pieces[0].shape, pieces[0].dtype)
+    for step, piece in enumerate(pieces):
+        column = lax.dynamic_update_index_in_dim(column, piece, (z - step) % depth, 0)
+    return column, shifted(column, "y", 1)
+
+
+def gather_across_cores(column, beside):
+    _, y, _ = places()
+    plane = jnp.stack(
+        [jnp.where(y == 0, column, beside), jnp.where(y == 0, beside, column)], axis=1
+    )
+    return plane, shifted(plane, "core", 1)
+
+
+def gathered_rows(plane, across):
+    _, _, core = places()
+    whole = jnp.stack(
+        [jnp.where(core == 0, plane, across), jnp.where(core == 0, across, plane)], axis=2
+    )
+    return whole.reshape((-1, whole.shape[-1]))
+
+
+def after(value, *deps):
+    return lax.optimization_barrier((value,) + deps)[0]
+
+
+def across_cores(full):
+    _, _, core = places()
+    depth = lax.axis_size("fsdp") // 4
+    grid = full.reshape(depth, 2, 2, -1, full.shape[1])
+    sent = jnp.where(core == 0, grid[:, :, 1], grid[:, :, 0])
+    kept = jnp.where(core == 0, grid[:, :, 0], grid[:, :, 1])
+    return kept, shifted(sent, "core", 1)
+
+
+def across_y(kept, came):
+    _, y, _ = places()
+
+    def summed(side):
+        part = jnp.where(side == 0, kept[:, 0], kept[:, 1]).astype(jnp.float32)
+        return part + jnp.where(side == 0, came[:, 0], came[:, 1]).astype(jnp.float32)
+
+    return summed(y), shifted(summed(1 - y).astype(jnp.bfloat16), "y", 1)
+
+
+def across_z(kept, came):
+    z, _, _ = places()
+    depth = kept.shape[0]
+    column = (kept + came.astype(jnp.float32)).astype(jnp.bfloat16)
+
+    def at(step):
+        return lax.dynamic_index_in_dim(column, (z + step) % depth, 0, keepdims=False)
+
+    return [at(0)] + [shifted(at(step), "z", step) for step in range(1, depth)]
+
+
+def summed_rows(pieces):
+    total = pieces[0].astype(jnp.float32)
+    for piece in pieces[1:]:
+        total = total + piece.astype(jnp.float32)
+    return total.astype(jnp.bfloat16)
+
+
+def section_backward(incoming, incoming_other, kept, w_qkv, weights, tables, attn_all=None):
+    w_out, w_up, _, gains = weights
+    w_down = kept["w_down"]
     tokens, width = incoming.shape
     starts, low, high = tables
     halo = halo_count()
+
+    def up_grad(rows, up_proj):
+        act_grad = contract(rows, w_down, 1, 1)
+        return jax.vjp(gelu_tanh, up_proj)[1](act_grad)[0].astype(jnp.bfloat16)
+
+    up_own = up_grad(incoming, kept["up_own"])
+    incoming_other, up_own = lax.optimization_barrier((incoming_other, up_own))
+    up_other = up_grad(incoming_other, kept["up_other"])
+    arrived = swap(contract(up_other, w_up, 1, 1).astype(jnp.bfloat16))
+    partial = contract(up_own, w_up, 1, 1)
+    up_low = jnp.concatenate([up_own, up_other])
     both = jnp.concatenate([incoming, incoming_other])
-    act_grad = contract(both, w_down, 1, 1)
-    unused_value, gelu_pull = jax.vjp(gelu_tanh, kept["up_proj"])
-    up_low = gelu_pull(act_grad)[0].astype(jnp.bfloat16)
-    partial = contract(up_low, w_up, 1, 1)
-    arrived = swap(partial[tokens:].astype(jnp.bfloat16)).astype(jnp.float32)
-    ffn_grad = partial[:tokens] + arrived
-    grad_down = scatter(contract(kept["act_low"], both, 0, 0))
     grad_up = contract(kept["ffn_both"], up_low, 0, 0).astype(jnp.bfloat16)
+    full_down = contract(kept["act_both"], both, 0, 0).astype(jnp.bfloat16)
+    arrived, partial = lax.optimization_barrier((arrived, partial, grad_up, full_down))[:2]
+    staged = lax.axis_size("fsdp") == H
+    if staged:
+        down_kept, down_came = across_cores(full_down)
+    ffn_grad = partial + arrived.astype(jnp.float32)
     resid_norm, gain_two, shift_two = norm_back(
         ffn_grad, kept["normed_two"], kept["scaled_two"], gains[width:]
     )
     resid_grad = incoming.astype(jnp.float32) + resid_norm
     proj_low = resid_grad.astype(jnp.bfloat16)
     mixed_grad = contract(w_out, proj_low, 1, 1).astype(jnp.bfloat16)
+    if staged:
+        down_kept, down_came = across_y(down_kept, after(down_came, mixed_grad))
     mixed_grad = exchange(mixed_grad.reshape(H, HD, tokens))
     grad_out = contract(kept["mixed"], proj_low, 1, 0).astype(jnp.bfloat16)
-    grad_mid = scatter(jnp.concatenate([grad_out, grad_up], axis=1))
+    grad_mid = jnp.concatenate([grad_out, grad_up], axis=1)
+    mixed_grad = after(mixed_grad, grad_mid)
+    grad_mid = scatter(grad_mid)
+    if staged:
+        grad_down = across_z(down_kept, after(down_came, mixed_grad))
+    else:
+        grad_down = [scatter(full_down)]
     dqkv = attend_back(
         kept["qkv"], starts, low, high, mixed_grad, kept["mixed_f32"], kept["lse"], halo
     )
@@ -309,10 +492,17 @@
         behind = from_group(dqkv[:halo], -1).astype(jnp.float32)
         behind = behind.at[:, :HD].set(0.0)
         dqkv = (dqkv[halo:].astype(jnp.float32) + behind).astype(jnp.bfloat16)
-    dqkv = exchange(dqkv)
-    dqkv = dqkv.reshape(H, 3, HD, tokens).transpose(1, 0, 2, 3).reshape(3 * H * HD, tokens)
+    own_head = dqkv
+    dqkv = from_heads(exchange(dqkv), tokens)
+    if staged:
+        dqkv = after(dqkv, *grad_down)
     attn_grad = contract(dqkv, w_qkv, 0, 1)
-    grad_qkv = scatter(contract(kept["attn_low"], dqkv, 0, 1))
+    if attn_all is None:
+        grad_qkv = scatter(contract(kept["attn_low"], dqkv, 0, 1))
+    else:
+        dims = (((0, 2), (0, 1)), ((), ()))
+        grad_head = lax.dot_general(own_head, attn_all, dims, preferred_element_type=jnp.float32)
+        grad_qkv = grad_head
     qkv_bias = jnp.sum(dqkv, axis=1, dtype=jnp.float32)
     input_norm, gain_one, shift_one = norm_back(
         attn_grad, kept["normed_one"], kept["scaled_one"], gains[:width]
@@ -330,12 +520,12 @@
     return resid_grad + input_norm, (grad_qkv, grad_mid, grad_down), vector_grad
 
 
-def body(x_in, cotangent, segment, w_qkv, w_out, w_up, w_down, vectors, gains):
+def whole_step(x_in, cotangent, segment, w_qkv, w_out, w_up, w_down, vectors, gains):
     pipe_index = lax.axis_index("pipe")
     fsdp_index = lax.axis_index("fsdp")
     count = lax.axis_size("fsdp")
     first = pipe_index == 0
-    batches, tokens, width = x_in.shape
+    _, _, width = x_in.shape
     hidden = w_up.shape[2]
     half = hidden // count // 2
 
@@ -381,27 +571,50 @@
             "down": flat[5 * width + hidden :],
         }
         gain_all = piece[:, vec_rows:].reshape(-1)
-        full_qkv = lax.all_gather(qkv_shards[section], "fsdp", axis=0, tiled=True)
         full_mid = lax.all_gather(mid_shards[section], "fsdp", axis=0, tiled=True)
-        full_down = lax.all_gather(down_shards[section], "fsdp", axis=0, tiled=True)
-        return full_qkv, full_mid[:, :width], full_mid[:, width:], full_down, named, gain_all
-
+        return full_mid[:, :width], full_mid[:, width:], named, gain_all
+
+    start_low = mine((x_in[0], x_in[1]))
+    start_all = lax.all_gather(start_low, "fsdp", axis_index_groups=head_groups())
+    w_head = spread_head_columns(qkv_shards[0])
     weights = [section_weights(0), section_weights(1)]
-    start = mine((x_in[0], x_in[1])).astype(jnp.float32)
-    result_zero, kept_zero = section_forward(start, weights[0], tables)
+    w_qkv_one = lax.all_gather(qkv_shards[1], "fsdp", axis=0, tiled=True)
+    w_qkv_zero = lax.all_gather(qkv_shards[0], "fsdp", axis=0, tiled=True)
+
+    def normed(features, section):
+        named, gain_all = weights[section][2:]
+        attn_in, normed_one, scaled_one = layer_norm(features, gain_all[:width], named["ln1"])
+        return attn_in.astype(jnp.bfloat16), normed_one, scaled_one
+
+    attn_all = normed(start_all.astype(jnp.float32), 0)[0]
+    qkv_zero = heads_of_group(attn_all, w_head, weights[0][2], fsdp_index % H)
+    start = start_low.astype(jnp.float32)
+    normed_start = normed(start, 0)
+    unfinished_zero, kept_zero = section_forward(
+        start, normed_start, qkv_zero, down_shards[0], weights[0], tables
+    )
+    result_zero = finish(unfinished_zero, ())[0]
     low_zero = result_zero.astype(jnp.bfloat16)
-    result_one, kept_one = section_forward(low_zero.astype(jnp.float32), weights[1], tables)
-    low_one = result_one.astype(jnp.bfloat16)
+    middle = low_zero.astype(jnp.float32)
+    normed_middle = normed(middle, 1)
+    qkv_one = heads_from_tokens(normed_middle[0], w_qkv_one, weights[1][2])
+    unfinished_one, kept_one = section_forward(
+        middle, normed_middle, qkv_one, down_shards[1], weights[1], tables
+    )
 
     pair = (cotangent[0], cotangent[1])
     grad_one, params_one, vecs_one = section_backward(
-        mine(pair), other(pair), kept_one, weights[1], tables
+        mine(pair), other(pair), kept_one, w_qkv_one, weights[1], tables
     )
     grad_one = grad_one.astype(jnp.bfloat16)
+    result_one, grad_one = finish(unfinished_one, grad_one)
+    low_one = result_one.astype(jnp.bfloat16)
     grad_zero, params_zero, vecs_zero = section_backward(
-        grad_one, swap(grad_one), kept_zero, weights[0], tables
+        grad_one, swap(grad_one), kept_zero, w_qkv_zero, weights[0], tables, attn_all
     )
     grad_zero = grad_zero.astype(jnp.bfloat16)
+    down_one = summed_rows(params_one[2])
+    down_zero = summed_rows(params_zero[2])
 
     def both_batches(zero, one):
         kept_rows = mine((zero, one))
@@ -413,21 +626,6 @@
 
     def owned(zero, one):
         return mine((zero, one)), swap(other((zero, one)))
-
-    qkv_mine, qkv_came = owned(params_zero[0], params_one[0])
-    mid_mine, mid_came = owned(params_zero[1], params_one[1])
-    down_mine, down_came = owned(params_zero[2], params_one[2])
-    grad_qkv = qkv_mine.astype(jnp.float32) + qkv_came.astype(jnp.float32)
-    grad_out = mid_mine[:, :width].astype(jnp.float32) + mid_came[:, :width].astype(jnp.float32)
-
-    def woven(kept_half, came_half):
-        return jnp.where(first, kept_half, came_half), jnp.where(first, came_half, kept_half)
-
-    rows = w_up.shape[1]
-    up_pair = woven(mid_mine[:, width:], mid_came[:, width:])
-    grad_up = jnp.stack([part.reshape(rows, count, half) for part in up_pair], axis=2)
-    grad_up = grad_up.reshape(rows, hidden).astype(jnp.float32)
-    grad_down = jnp.concatenate(woven(down_mine, down_came)).astype(jnp.float32)
 
     def flat_vectors(named):
         up_half = named["up"].reshape(count, half)
@@ -439,7 +637,22 @@
         return jnp.concatenate([flat.reshape(count, -1), named["gains"].reshape(count, -1)], axis=1)
 
     small_grads = jnp.concatenate([flat_vectors(vecs_zero), flat_vectors(vecs_one)], axis=1)
-    small_grads = jnp.sum(lax.all_to_all(small_grads, "fsdp", 0, 0, tiled=True), axis=0)
+    qkv_zero_grad, small_grads = collect_head_columns(params_zero[0], small_grads)
+    qkv_mine, qkv_came = owned(qkv_zero_grad, params_one[0])
+    mid_mine, mid_came = owned(params_zero[1], params_one[1])
+    down_mine, down_came = owned(down_zero, down_one)
+    grad_qkv = qkv_mine.astype(jnp.float32) + qkv_came.astype(jnp.float32)
+    grad_out = mid_mine[:, :width].astype(jnp.float32) + mid_came[:, :width].astype(jnp.float32)
+
+    def woven(kept_half, came_half):
+        return jnp.where(first, kept_half, came_half), jnp.where(first, came_half, kept_half)
+
+    rows = w_up.shape[1]
+    up_pair = woven(mid_mine[:, width:], mid_came[:, width:])
+    grad_up = jnp.stack([part.reshape(rows, count, half) for part in up_pair], axis=2)
+    grad_up = grad_up.reshape(rows, hidden).astype(jnp.float32)
+    grad_down = jnp.concatenate(woven(down_mine, down_came)).astype(jnp.float32)
+
     small_mine, small_came = owned(small_grads[:lengths], small_grads[lengths:])
     small_total = small_mine + small_came
     return (
@@ -456,7 +669,7 @@
 
 def solution(mesh):
     return jax.shard_map(
-        body,
+        whole_step,
         mesh=mesh,
         in_specs=(
             P(None, "fsdp", None),

time: 1090 us -> 910 us (0.83)
  blocking collectives: 229 us -> 84.3 us
  waiting for transfers between devices: 457 us -> 350 us
  other arithmetic: 42.1 us -> 99.5 us
  starting transfers between devices: 85.2 us -> 117 us
  matrix products: 120 us -> 91.3 us
    all_to_all x4 -> x1, blocking collectives: 206 us -> 61.4 us  [exchange(): lax.all_to_all(blocks, 'fsdp', 0, 0, axis_index_groups=head_groups(), til...]
    reduce_scatter x6 -> x3, waiting for transfers between devices: 192 us -> 54.1 us  [scatter(): lax.psum_scatter(grad.astype(jnp.bfloat16), 'fsdp', scatter_dimension=0,...]
    ppermute x0 -> x20, waiting for transfers between devices: none -> 125 us  [shifted(): return lax.ppermute(value, 'fsdp', [(i, ahead(i)) for i in range(count)])]
    ppermute x17, waiting for transfers between devices: 132 us -> 83.7 us  [swap(): return lax.ppermute(value, 'pipe', [(0, 1), (1, 0)])]
    dot_general x24 -> x31, matrix products: 120 us -> 86 us  [contract(): lax.dot_general(left, right, dims, preferred_element_type=jnp.float32)]
    ppermute x0 -> x20, starting transfers between devices: none -> 31.8 us  [shifted(): return lax.ppermute(value, 'fsdp', [(i, ahead(i)) for i in range(count)])]
    all_gather x4 -> x3, waiting for transfers between devices: 52.7 us -> 29.5 us  [the longest x1 17.5 us: whole_step(): w_qkv_one = lax.all_gather(qkv_shards[1], 'fsdp', axis=0, tiled=True)]
    convert_element_type x3 -> x9, other arithmetic: 1.18 us -> 21.3 us  [the longest x2 7.7 us: across_y(): return (summed(y), shifted(summed(1 - y).astype(jnp.bfloat16), 'y', 1))]
  transfers between devices with their start and end apart: 34 -> 53, of which waited for: 25 -> 26; matrix products, arithmetic and copies ran while one was open for 14% -> 23% of each run, Pallas kernels for 11% -> 12%
where the time goes in v2:
time: 910 us; the launch traced here: 900 us
  waiting for transfers between devices  350 us (38%)
  starting transfers between devices  117 us (13%)
  Pallas kernels  111 us (12%)
  other arithmetic  99.5 us (11%)
  matrix products  91.3 us (10%)
  blocking collectives  84.3 us (9%)
  local copies, waits for them, and re-layouts  30.5 us (3%)
  between operations  16.4 us (2%)
    ppermute x20, waiting for transfers between devices, shifted(): return lax.ppermute(value, 'fsdp', [(i, ahead(i)) for i in range(count)])  125 us
    dot_general x31, matrix products, contract(): lax.dot_general(left, right, dims, preferred_element_type=jnp.float32)  86 us
    ppermute x17, waiting for transfers between devices, swap(): return lax.ppermute(value, 'pipe', [(0, 1), (1, 0)])  83.7 us
    pallas_call x2, Pallas kernels, attend_back(): pl.pallas_call(functools.partial(backward_kernel, off), out_shape=jax.Sha...  69.5 us
    all_to_all x1, blocking collectives, exchange(): lax.all_to_all(blocks, 'fsdp', 0, 0, axis_index_groups=head_groups(), til...  61.4 us
    all_to_all x6, waiting for transfers between devices, exchange(): lax.all_to_all(blocks, 'fsdp', 0, 0, axis_index_groups=head_groups(), til...  57.5 us
    all_to_all x6, starting transfers between devices, exchange(): lax.all_to_all(blocks, 'fsdp', 0, 0, axis_index_groups=head_groups(), til...  56 us
    reduce_scatter x3, waiting for transfers between devices, scatter(): lax.psum_scatter(grad.astype(jnp.bfloat16), 'fsdp', scatter_dimension=0,...  54.1 us
  transfers between devices with their start and end apart: 53, of which 26 were waited for; matrix products, arithmetic and copies ran while one was open for 23% of the time, Pallas kernels for 12%

profile of v2, /device:TPU:0, one launch (start us, length us, event | category | flops | bytes accessed | tf_op | source)
XLA Modules:
  0.0 900.4 jit_solution(5159329395412416041)
XLA Ops:
  14.5 9.0 %collective-permute-done.6 = bf16[64,3072]{1,0:T(8,128)(2,1)S(1)} collective-permute-done((bf16[64,3072]{1,0:T(8,128)(2,1)S(1)}, bf16[64,3072]{1,0:T(8,128)(2,1)S(1)}, u32[]{:S(2)}, u32[]{:S(2)}) %collective-permute-start.6) | collective-permute-done | bytes 393248 | tf_op jit(solution)/shard_map/ppermute | solution.py:206
  26.5 8.5 collective-permute-done.1
  39.6 22.8 %all-gather.1 = bf16[16,1,1792]{2,1,0:T(2,128)(2,1)S(1)} all-gather(bf16[1,1,1792]{2,1,0:T(2,128)(2,1)S(1)} %reshape.499), channel_id=2, replica_groups=mesh['pipe'=2,'fsdp'=16] {'fsdp'}, dimensions={0}, use_global_device_ids=true | all-gather | bytes 60928 | tf_op jit(solution)/shard_map/all_gather | solution.py:554
  63.2 9.1 %convert_reduce_fusion = s32[4096]{0:T(1024)S(1)} fusion(s32[4096]{0:T(1024)S(1)} %bitcast.370), kind=kLoop, calls=%fused_computation | loop fusion | flops 50327552 | bytes 32768 | tf_op jit(solution)/shard_map/reduce_sum | solution.py:241
  80.8 12.0 %all-gather.8.cloned.1.call-done = bf16[16,256,1024]{2,1,0:T(8,128)(2,1)} async-done(((bf16[1,256,1024]{2,1,0:T(8,128)(2,1)}), bf16[16,256,1024]{2,1,0:T(8,128)(2,1)}) %all-gather.8.cloned.1.call-update) | async-done | bytes 8388624 | tf_op jit(solution)/shard_map/all_gather | solution.py:578
  106.8 6.4 fusion.6
  119.1 20.9 %attend.2 = (bf16[16,64,256]{2,1,0:T(8,128)(2,1)}, f32[16,64,256]{2,1,0:T(8,128)}, f32[16,1,256]{2,1,0:T(1,128)}) custom-call(s32[16]{0:T(128)} %and_select_fusion.low_ref, bf16[16,192,256]{2,1,0:T(8,128)(2,1)} %bitcast.317, s32[16,1,256]{2,1,0:T(1,128)} %bitcast.361), custom_call_target="tpu_custom_call" | custom-call | tf_op jit(solution)/shard_map/attend/pallas_call | solution.py:87
  140.3 16.7 %all-to-all-start.1 = ((bf16[16,64,256]{2,1,0:T(8,128)(2,1)}), bf16[16,64,256]{2,1,0:T(8,128)(2,1)S(1)}, u32[]{:S(2)}, u32[]{:S(2)}) async-start(bf16[16,64,256]{2,1,0:T(8,128)(2,1)} %get-tuple-element.62), calls=%async_computation.1 | async-start | bytes 1048576 | tf_op jit(solution)/shard_map/all_to_all | solution.py:217
  157.7 22.7 %all-to-all-done.1 = bf16[16,64,256]{2,1,0:T(8,128)(2,1)S(1)} async-done(((bf16[16,64,256]{2,1,0:T(8,128)(2,1)}), bf16[16,64,256]{2,1,0:T(8,128)(2,1)S(1)}, u32[]{:S(2)}, u32[]{:S(2)}) %all-to-all-start.1) | async-done | bytes 524320 | tf_op jit(solution)/shard_map/all_to_all | solution.py:217
  192.9 9.7 %collective-permute-done.7 = bf16[256,1024]{1,0:T(8,128)(2,1)S(1)} collective-permute-done((bf16[256,1024]{1,0:T(8,128)(2,1)S(1)}, bf16[256,1024]{1,0:T(8,128)(2,1)S(1)}, u32[]{:S(2)}, u32[]{:S(2)}) %collective-permute-start.7) | collective-permute-done | bytes 524320 | tf_op jit(solution)/shard_map/ppermute | solution.py:206
  212.3 10.7 %collective-permute-done.10 = bf16[256,1024]{1,0:T(8,128)(2,1)S(1)} collective-permute-done((bf16[256,1024]{1,0:T(8,128)(2,1)S(1)}, bf16[256,1024]{1,0:T(8,128)(2,1)S(1)}, u32[]{:S(2)}, u32[]{:S(2)}) %collective-permute-start.10) | collective-permute-done | bytes 524320 | tf_op jit(solution)/shard_map/ppermute | solution.py:206
  223.5 17.5 %all-gather.12.cloned.1.call-done = bf16[1024,3072]{1,0:T(8,128)(2,1)} async-done(((bf16[64,3072]{1,0:T(8,128)(2,1)}), bf16[1024,3072]{1,0:T(8,128)(2,1)}) %all-gather.12.cloned.1.call-update) | async-done | bytes 6291472 | tf_op jit(solution)/shard_map/all_gather | solution.py:581
  246.3 61.4 %all_to_all.45.qkv_ref = bf16[16,192,256]{2,1,0:T(8,128)(2,1)} all-to-all(bf16[16,192,256]{2,1,0:T(8,128)(2,1)S(1)} %bitcast.325), channel_id=1, replica_groups=mesh['pipe'=2,'fsdp'=16] {'fsdp'}, dimensions={0} | all-to-all | bytes 3145728 | tf_op jit(solution)/shard_map/all_to_all | solution.py:217
  319.0 20.9 %attend.3 = (bf16[16,64,256]{2,1,0:T(8,128)(2,1)}, f32[16,64,256]{2,1,0:T(8,128)}, f32[16,1,256]{2,1,0:T(1,128)}) custom-call(s32[16]{0:T(128)} %and_select_fusion.low_ref, bf16[16,192,256]{2,1,0:T(8,128)(2,1)} %all_to_all.45.qkv_ref, s32[16,1,256]{2,1,0:T(1,128)} %bitcast.362), custom_call_target="tpu_custom_call" | custom-call | tf_op jit(solution)/shard_map/attend/pallas_call | solution.py:87
  345.7 8.4 all-to-all-start.3
  356.8 17.9 %all-to-all-done.3 = bf16[16,64,256]{2,1,0:T(8,128)(2,1)S(1)} async-done(((bf16[16,64,256]{2,1,0:T(8,128)(2,1)}), bf16[16,64,256]{2,1,0:T(8,128)(2,1)S(1)}, u32[]{:S(2)}, u32[]{:S(2)}) %all-to-all-start.3) | async-done | bytes 524320 | tf_op jit(solution)/shard_map/all_to_all | solution.py:217
  385.6 10.9 %collective-permute-done.14 = bf16[256,1024]{1,0:T(8,128)(2,1)S(1)} collective-permute-done((bf16[256,1024]{1,0:T(8,128)(2,1)S(1)}, bf16[256,1024]{1,0:T(8,128)(2,1)S(1)}, u32[]{:S(2)}, u32[]{:S(2)}) %collective-permute-start.14) | collective-permute-done | bytes 524320 | tf_op jit(solution)/shard_map/ppermute | solution.py:206
  424.3 10.3 %all-to-all-start.4 = ((bf16[16,64,256]{2,1,0:T(8,128)(2,1)}), bf16[16,64,256]{2,1,0:T(8,128)(2,1)}, u32[]{:S(2)}, u32[]{:S(2)}) async-start(bf16[16,64,256]{2,1,0:T(8,128)(2,1)} %bitcast.356), calls=%async_computation.4 | async-start | bytes 1048576 | tf_op jit(solution)/shard_map/all_to_all | solution.py:217
  442.6 11.2 %all-to-all-done.4.do_ref = bf16[16,64,256]{2,1,0:T(8,128)(2,1)} async-done(((bf16[16,64,256]{2,1,0:T(8,128)(2,1)}), bf16[16,64,256]{2,1,0:T(8,128)(2,1)}, u32[]{:S(2)}, u32[]{:S(2)}) %all-to-all-start.4) | async-done | bytes 524320 | tf_op jit(solution)/shard_map/all_to_all | solution.py:217
  453.8 34.8 %attend_back.2 = bf16[16,192,256]{2,1,0:T(8,128)(2,1)} custom-call(s32[16]{0:T(128)} %and_select_fusion.low_ref, s32[16]{0:T(128)} %broadcast_add_fusion.high_ref, bf16[16,192,256]{2,1,0:T(8,128)(2,1)} %all_to_all.45.qkv_ref, s32[16,1,256]{2,1,0:T(1,128)} %bitcast.363, bf16[16,64,256]{2,1,0:T(8,128)(2,1)} %all-to-all-done.4.do_ref, ...), custom_call_target="tpu_custom_call" | custom-call | tf_op jit(solution)/shard_map/attend_back/pallas_call | solution.py:161
  502.4 33.9 %collective-permute-done.20 = bf16[4,128,1024]{2,1,0:T(8,128)(2,1)} collective-permute-done((bf16[4,128,1024]{2,1,0:T(8,128)(2,1)}, bf16[4,128,1024]{2,1,0:T(8,128)(2,1)}, u32[]{:S(2)}, u32[]{:S(2)}) %collective-permute-start.20) | collective-permute-done | bytes 1048608 | tf_op jit(solution)/shard_map/ppermute | solution.py:367
  552.4 9.8 %collective-permute-done.22 = bf16[128,1024]{1,0:T(8,128)(2,1)} collective-permute-done((bf16[128,1024]{1,0:T(8,128)(2,1)}, bf16[128,1024]{1,0:T(8,128)(2,1)}, u32[]{:S(2)}, u32[]{:S(2)}) %collective-permute-start.22) | collective-permute-done | bytes 262176 | tf_op jit(solution)/shard_map/ppermute | solution.py:367
  588.9 9.7 %collective-permute-done.25 = bf16[256,1024]{1,0:T(8,128)(2,1)S(1)} collective-permute-done((bf16[256,1024]{1,0:T(8,128)(2,1)S(1)}, bf16[256,1024]{1,0:T(8,128)(2,1)S(1)}, u32[]{:S(2)}, u32[]{:S(2)}) %collective-permute-start.25) | collective-permute-done | bytes 524320 | tf_op jit(solution)/shard_map/ppermute | solution.py:206
  617.1 9.4 %all-to-all-start.6 = ((bf16[16,64,256]{2,1,0:T(8,128)(2,1)}), bf16[16,64,256]{2,1,0:T(8,128)(2,1)}, u32[]{:S(2)}, u32[]{:S(2)}) async-start(bf16[16,64,256]{2,1,0:T(8,128)(2,1)} %bitcast.69), calls=%async_computation.6 | async-start | bytes 1048576 | tf_op jit(solution)/shard_map/all_to_all | solution.py:217
  637.8 5.7 all-to-all-done.6.do_ref
  643.5 34.7 %attend_back.3 = bf16[16,192,256]{2,1,0:T(8,128)(2,1)} custom-call(s32[16]{0:T(128)} %and_select_fusion.low_ref, s32[16]{0:T(128)} %broadcast_add_fusion.high_ref, bf16[16,192,256]{2,1,0:T(8,128)(2,1)} %bitcast.318, s32[16,1,256]{2,1,0:T(1,128)} %bitcast.364, bf16[16,64,256]{2,1,0:T(8,128)(2,1)} %all-to-all-done.6.do_ref, ...), custom_call_target="tpu_custom_call" | custom-call | tf_op jit(solution)/shard_map/attend_back/pallas_call | solution.py:161
  678.2 5.8 all-to-all-start.7
  691.7 51.7 %collective-permute-done.28 = bf16[4,128,1024]{2,1,0:T(8,128)(2,1)} collective-permute-done((bf16[4,128,1024]{2,1,0:T(8,128)(2,1)}, bf16[4,128,1024]{2,1,0:T(8,128)(2,1)}, u32[]{:S(2)}, u32[]{:S(2)}) %collective-permute-start.28) | collective-permute-done | bytes 1048608 | tf_op jit(solution)/shard_map/ppermute | solution.py:367
  761.0 21.4 %collective-permute-done.30 = bf16[128,1024]{1,0:T(8,128)(2,1)} collective-permute-done((bf16[128,1024]{1,0:T(8,128)(2,1)S(1)}, bf16[128,1024]{1,0:T(8,128)(2,1)}, u32[]{:S(2)}, u32[]{:S(2)}) %collective-permute-start.30) | collective-permute-done | bytes 262176 | tf_op jit(solution)/shard_map/ppermute | solution.py:367
  806.4 10.3 %collective-permute-done.32 = bf16[256,1024]{1,0:T(8,128)(2,1)S(1)} collective-permute-done((bf16[256,1024]{1,0:T(8,128)(2,1)S(1)}, bf16[256,1024]{1,0:T(8,128)(2,1)S(1)}, u32[]{:S(2)}, u32[]{:S(2)}) %collective-permute-start.32) | collective-permute-done | bytes 524320 | tf_op jit(solution)/shard_map/ppermute | solution.py:206
  824.0 54.1 %reduce-scatter.6.cloned.1.call-done = bf16[64,3072]{1,0:T(8,128)(2,1)} async-done(((bf16[1024,3072]{1,0:T(8,128)(2,1)}), bf16[64,3072]{1,0:T(8,128)(2,1)}) %reduce-scatter.6.cloned.1.call-update) | async-done | bytes 393232 | tf_op jit(solution)/shard_map/reduce_scatter | solution.py:356
  881.9 7.6 collective-permute-done.34
  (467 shorter events, 287.9 us)
Async XLA Ops:
  7.2 85.6 %all-gather.8.cloned.1.call-start = ((), (), s32[]{:S(2)}) async-start(), calls=%async_computation.12 | async-start | bytes 8912896 | tf_op jit(solution)/shard_map/all_gather | solution.py:578
  10.0 174.9 %all-gather.10.cloned.1.call-start = ((), (), s32[]{:S(2)}) async-start(), calls=%async_computation.13 | async-start | bytes 6684672 | tf_op jit(solution)/shard_map/all_gather | solution.py:574
  24.6 216.4 %all-gather.12.cloned.1.call-start = ((), (), s32[]{:S(2)}) async-start(), calls=%async_computation.14 | async-start | bytes 6684672 | tf_op jit(solution)/shard_map/all_gather | solution.py:581
  37.5 36.6 %collective-permute-start.2 = (bf16[128,1024]{1,0:T(8,128)(2,1)S(1)}, bf16[128,1024]{1,0:T(8,128)(2,1)S(1)}, u32[]{:S(2)}, u32[]{:S(2)}) collective-permute-start(bf16[128,1024]{1,0:T(8,128)(2,1)S(1)} %select_bitcast_fusion.20), channel_id=1, source_target_pairs={{0,16},{16,0},{1,17},{17,1},{2,18},{18,2},{3,19},{19,3},{4,20},{20... | collective-permute-start | bytes 786440 | tf_op jit(solution)/shard_map/ppermute | solution.py:206
  77.3 29.5 %all-to-all-start = ((bf16[16,192,64]{1,2,0:T(8,128)(2,1)}), bf16[16,192,64]{1,2,0:T(8,128)(2,1)S(1)}, u32[]{:S(2)}, u32[]{:S(2)}) async-start(bf16[16,192,64]{1,2,0:T(8,128)(2,1)} %copy.167), calls=%async_computation | async-start | bytes 1048576 | tf_op jit(solution)/shard_map/all_to_all | solution.py:267
  114.5 25.6 %collective-permute-start.3 = (bf16[128,1024]{1,0:T(8,128)(2,1)S(1)}, bf16[128,1024]{1,0:T(8,128)(2,1)S(1)}, u32[]{:S(2)}, u32[]{:S(2)}) collective-permute-start(bf16[128,1024]{1,0:T(8,128)(2,1)S(1)} %get-tuple-element.58), channel_id=1, source_target_pairs={{0,4},{1,5},{2,6},{3,7},{4,8},{5,9},{6,10},{7,11},{8,12},{9,13},{1... | collective-permute-start | bytes 786440 | tf_op jit(solution)/shard_map/ppermute | solution.py:367
  114.5 25.6 %collective-permute-start.4 = (bf16[128,1024]{1,0:T(8,128)(2,1)S(1)}, bf16[128,1024]{1,0:T(8,128)(2,1)S(1)}, u32[]{:S(2)}, u32[]{:S(2)}) collective-permute-start(bf16[128,1024]{1,0:T(8,128)(2,1)S(1)} %get-tuple-element.58), channel_id=1, source_target_pairs={{0,8},{1,9},{2,10},{3,11},{4,12},{5,13},{6,14},{7,15},{8,0},{9,1},... | collective-permute-start | bytes 786440 | tf_op jit(solution)/shard_map/ppermute | solution.py:367
  114.5 25.6 %collective-permute-start.5 = (bf16[128,1024]{1,0:T(8,128)(2,1)S(1)}, bf16[128,1024]{1,0:T(8,128)(2,1)S(1)}, u32[]{:S(2)}, u32[]{:S(2)}) collective-permute-start(bf16[128,1024]{1,0:T(8,128)(2,1)S(1)} %get-tuple-element.58), channel_id=1, source_target_pairs={{0,12},{1,13},{2,14},{3,15},{4,0},{5,1},{6,2},{7,3},{8,4},{9,5},{1... | collective-permute-start | bytes 786440 | tf_op jit(solution)/shard_map/ppermute | solution.py:367
  140.2 40.1 %collective-permute-start.8 = (bf16[4,128,1024]{2,1,0:T(8,128)(2,1)S(1)}, bf16[4,128,1024]{2,1,0:T(8,128)(2,1)S(1)}, u32[]{:S(2)}, u32[]{:S(2)}) collective-permute-start(bf16[4,128,1024]{2,1,0:T(8,128)(2,1)S(1)} %bitcast_dynamic-update-slice_fusion.4), channel_id=1, source_target_pairs={{0,2},{1,3},{2,0},{3,1},{4,6},{5,7},{6,4},{7,5},{8,10},{9,11},{10,... | collective-permute-start | bytes 3145736 | tf_op jit(solution)/shard_map/ppermute | solution.py:367
  140.3 40.0 %all-to-all-start.1 = ((bf16[16,64,256]{2,1,0:T(8,128)(2,1)}), bf16[16,64,256]{2,1,0:T(8,128)(2,1)S(1)}, u32[]{:S(2)}, u32[]{:S(2)}) async-start(bf16[16,64,256]{2,1,0:T(8,128)(2,1)} %get-tuple-element.62), calls=%async_computation.1 | async-start | bytes 1048576 | tf_op jit(solution)/shard_map/all_to_all | solution.py:217
  157.1 221.9 %all-gather.14.cloned.1.call-start = ((), (), s32[]{:S(2)}) async-start(), calls=%async_computation.15 | async-start | bytes 6684672 | tf_op jit(solution)/shard_map/all_gather | solution.py:574
  307.7 34.0 %collective-permute-start.11 = (bf16[128,1024]{1,0:T(8,128)(2,1)S(1)}, bf16[128,1024]{1,0:T(8,128)(2,1)S(1)}, u32[]{:S(2)}, u32[]{:S(2)}) collective-permute-start(bf16[128,1024]{1,0:T(8,128)(2,1)S(1)} %copy-done.44), channel_id=1, source_target_pairs={{0,4},{1,5},{2,6},{3,7},{4,8},{5,9},{6,10},{7,11},{8,12},{9,13},{1... | collective-permute-start | bytes 786440 | tf_op jit(solution)/shard_map/ppermute | solution.py:367
  312.8 29.0 %collective-permute-start.12 = (bf16[128,1024]{1,0:T(8,128)(2,1)S(1)}, bf16[128,1024]{1,0:T(8,128)(2,1)S(1)}, u32[]{:S(2)}, u32[]{:S(2)}) collective-permute-start(bf16[128,1024]{1,0:T(8,128)(2,1)S(1)} %copy-done.44), channel_id=1, source_target_pairs={{0,8},{1,9},{2,10},{3,11},{4,12},{5,13},{6,14},{7,15},{8,0},{9,1},... | collective-permute-start | bytes 786440 | tf_op jit(solution)/shard_map/ppermute | solution.py:367
  315.7 26.1 %collective-permute-start.13 = (bf16[128,1024]{1,0:T(8,128)(2,1)S(1)}, bf16[128,1024]{1,0:T(8,128)(2,1)S(1)}, u32[]{:S(2)}, u32[]{:S(2)}) collective-permute-start(bf16[128,1024]{1,0:T(8,128)(2,1)S(1)} %copy-done.44), channel_id=1, source_target_pairs={{0,12},{1,13},{2,14},{3,15},{4,0},{5,1},{6,2},{7,3},{8,4},{9,5},{1... | collective-permute-start | bytes 786440 | tf_op jit(solution)/shard_map/ppermute | solution.py:367
  343.9 30.8 %collective-permute-start.15 = (bf16[4,128,1024]{2,1,0:T(8,128)(2,1)}, bf16[4,128,1024]{2,1,0:T(8,128)(2,1)}, u32[]{:S(2)}, u32[]{:S(2)}) collective-permute-start(bf16[4,128,1024]{2,1,0:T(8,128)(2,1)} %bitcast_dynamic-update-slice_fusion), channel_id=1, source_target_pairs={{0,2},{1,3},{2,0},{3,1},{4,6},{5,7},{6,4},{7,5},{8,10},{9,11},{10,... | collective-permute-start | bytes 3145736 | tf_op jit(solution)/shard_map/ppermute | solution.py:367
  345.7 28.9 %all-to-all-start.3 = ((bf16[16,64,256]{2,1,0:T(8,128)(2,1)}), bf16[16,64,256]{2,1,0:T(8,128)(2,1)S(1)}, u32[]{:S(2)}, u32[]{:S(2)}) async-start(bf16[16,64,256]{2,1,0:T(8,128)(2,1)} %get-tuple-element.76), calls=%async_computation.3 | async-start | bytes 1048576 | tf_op jit(solution)/shard_map/all_to_all | solution.py:217
  354.2 434.0 %all-gather.16.cloned.1.call-start = ((), (), s32[]{:S(2)}) async-start(), calls=%async_computation.16 | async-start | bytes 6684672 | tf_op jit(solution)/shard_map/all_gather | solution.py:582
  419.7 76.7 %collective-permute-start.19 = (bf16[4,2,128,1024]{3,2,1,0:T(8,128)(2,1)}, bf16[4,2,128,1024]{3,2,1,0:T(8,128)(2,1)}, u32[]{:S(2)}, u32[]{:S(2)}) collective-permute-start(bf16[4,2,128,1024]{3,2,1,0:T(8,128)(2,1)} %get-tuple-element.139), channel_id=1, source_target_pairs={{0,1},{1,0},{2,3},{3,2},{4,5},{5,4},{6,7},{7,6},{8,9},{9,8},{10,11... | collective-permute-start | bytes 6291464 | tf_op jit(solution)/shard_map/ppermute | solution.py:367
  424.3 29.5 %all-to-all-start.4 = ((bf16[16,64,256]{2,1,0:T(8,128)(2,1)}), bf16[16,64,256]{2,1,0:T(8,128)(2,1)}, u32[]{:S(2)}, u32[]{:S(2)}) async-start(bf16[16,64,256]{2,1,0:T(8,128)(2,1)} %bitcast.356), calls=%async_computation.4 | async-start | bytes 1048576 | tf_op jit(solution)/shard_map/all_to_all | solution.py:217
  488.6 58.2 %all-to-all-start.5 = ((bf16[16,192,256]{2,1,0:T(8,128)(2,1)}), bf16[16,192,256]{2,1,0:T(8,128)(2,1)}, u32[]{:S(2)}, u32[]{:S(2)}) async-start(bf16[16,192,256]{2,1,0:T(8,128)(2,1)} %attend_back.2), calls=%async_computation.5 | async-start | bytes 3145728 | tf_op jit(solution)/shard_map/all_to_all | solution.py:217
  493.9 328.8 %reduce-scatter.4.cloned.1.call-start = ((), (), s32[]{:S(2)}) async-start(), calls=%async_computation.17 | async-start | bytes 6684672 | tf_op jit(solution)/shard_map/reduce_scatter | solution.py:356
  500.6 35.8 %collective-permute-start.20 = (bf16[4,128,1024]{2,1,0:T(8,128)(2,1)}, bf16[4,128,1024]{2,1,0:T(8,128)(2,1)}, u32[]{:S(2)}, u32[]{:S(2)}) collective-permute-start(bf16[4,128,1024]{2,1,0:T(8,128)(2,1)} %fusion.137), channel_id=1, source_target_pairs={{0,2},{1,3},{2,0},{3,1},{4,6},{5,7},{6,4},{7,5},{8,10},{9,11},{10,... | collective-permute-start | bytes 3145736 | tf_op jit(solution)/shard_map/ppermute | solution.py:367
  566.9 257.1 %reduce-scatter.8.cloned.1.call-start = ((), (), s32[]{:S(2)}) async-start(), calls=%async_computation.19 | async-start | bytes 6684672 | tf_op jit(solution)/shard_map/reduce_scatter | solution.py:356
  613.0 71.0 %collective-permute-start.27 = (bf16[4,2,128,1024]{3,2,0,1:T(8,128)(2,1)}, bf16[4,2,128,1024]{3,2,0,1:T(8,128)(2,1)}, u32[]{:S(2)}, u32[]{:S(2)}) collective-permute-start(bf16[4,2,128,1024]{3,2,0,1:T(8,128)(2,1)} %get-tuple-element.134), channel_id=1, source_target_pairs={{0,1},{1,0},{2,3},{3,2},{4,5},{5,4},{6,7},{7,6},{8,9},{9,8},{10,11... | collective-permute-start | bytes 6291464 | tf_op jit(solution)/shard_map/ppermute | solution.py:367
  617.1 26.3 %all-to-all-start.6 = ((bf16[16,64,256]{2,1,0:T(8,128)(2,1)}), bf16[16,64,256]{2,1,0:T(8,128)(2,1)}, u32[]{:S(2)}, u32[]{:S(2)}) async-start(bf16[16,64,256]{2,1,0:T(8,128)(2,1)} %bitcast.69), calls=%async_computation.6 | async-start | bytes 1048576 | tf_op jit(solution)/shard_map/all_to_all | solution.py:217
  626.5 251.6 %reduce-scatter.6.cloned.1.call-start = ((), (), s32[]{:S(2)}) async-start(), calls=%async_computation.18 | async-start | bytes 6684672 | tf_op jit(solution)/shard_map/reduce_scatter | solution.py:356
  635.9 164.9 %collective-permute-start.24 = (bf16[256,1024]{1,0:T(8,128)(2,1)}, bf16[256,1024]{1,0:T(8,128)(2,1)}, u32[]{:S(2)}, u32[]{:S(2)}) collective-permute-start(bf16[256,1024]{1,0:T(8,128)(2,1)} %get-tuple-element.130), channel_id=1, source_target_pairs={{0,16},{16,0},{1,17},{17,1},{2,18},{18,2},{3,19},{19,3},{4,20},{20... | collective-permute-start | bytes 1572872 | tf_op jit(solution)/shard_map/ppermute | solution.py:206
  678.2 106.7 %all-to-all-start.7 = ((bf16[16,192,256]{2,1,0:T(8,128)(2,1)}), bf16[16,192,256]{2,1,0:T(8,128)(2,1)}, u32[]{:S(2)}, u32[]{:S(2)}) async-start(bf16[16,192,256]{2,1,0:T(8,128)(2,1)} %attend_back.3), calls=%async_computation.7 | async-start | bytes 3145728 | tf_op jit(solution)/shard_map/all_to_all | solution.py:217
  687.6 55.8 %collective-permute-start.28 = (bf16[4,128,1024]{2,1,0:T(8,128)(2,1)}, bf16[4,128,1024]{2,1,0:T(8,128)(2,1)}, u32[]{:S(2)}, u32[]{:S(2)}) collective-permute-start(bf16[4,128,1024]{2,1,0:T(8,128)(2,1)} %fusion.136), channel_id=1, source_target_pairs={{0,2},{1,3},{2,0},{3,1},{4,6},{5,7},{6,4},{7,5},{8,10},{9,11},{10,... | collective-permute-start | bytes 3145736 | tf_op jit(solution)/shard_map/ppermute | solution.py:367
  750.8 31.6 %collective-permute-start.30 = (bf16[128,1024]{1,0:T(8,128)(2,1)S(1)}, bf16[128,1024]{1,0:T(8,128)(2,1)}, u32[]{:S(2)}, u32[]{:S(2)}) collective-permute-start(bf16[128,1024]{1,0:T(8,128)(2,1)S(1)} %get-tuple-element.160), channel_id=1, source_target_pairs={{0,8},{1,9},{2,10},{3,11},{4,12},{5,13},{6,14},{7,15},{8,0},{9,1},... | collective-permute-start | bytes 786440 | tf_op jit(solution)/shard_map/ppermute | solution.py:367
  750.8 31.6 %collective-permute-start.29 = (bf16[128,1024]{1,0:T(8,128)(2,1)S(1)}, bf16[128,1024]{1,0:T(8,128)(2,1)}, u32[]{:S(2)}, u32[]{:S(2)}) collective-permute-start(bf16[128,1024]{1,0:T(8,128)(2,1)S(1)} %get-tuple-element.158), channel_id=1, source_target_pairs={{0,4},{1,5},{2,6},{3,7},{4,8},{5,9},{6,10},{7,11},{8,12},{9,13},{1... | collective-permute-start | bytes 786440 | tf_op jit(solution)/shard_map/ppermute | solution.py:367
  823.9 56.9 %collective-permute-start.33 = (bf16[64,3072]{1,0:T(8,128)(2,1)S(1)}, bf16[64,3072]{1,0:T(8,128)(2,1)S(1)}, u32[]{:S(2)}, u32[]{:S(2)}) collective-permute-start(bf16[64,3072]{1,0:T(8,128)(2,1)S(1)} %bitcast_select_fusion.2), channel_id=1, source_target_pairs={{0,16},{16,0},{1,17},{17,1},{2,18},{18,2},{3,19},{19,3},{4,20},{20... | collective-permute-start | bytes 1179656 | tf_op jit(solution)/shard_map/ppermute | solution.py:206
  (105 other events, 1107.6 us)
Sparse Core Ops, SparseCore 0:
  10.7 82.0 all-gather.7
  95.1 82.0 all-gather.9
  179.4 61.5 all-gather.11
  243.2 101.0 all-gather.13
  378.9 76.2 all-gather.15
  567.0 95.6 reduce-scatter.3
  666.7 124.1 reduce-scatter.7
  794.8 83.3 reduce-scatter.5
